TPU v7x, 256 devices: a whole 4x4x8 slice. The times are simulated.
256 devices in a mesh: lst: 8 (over y, core), chan: 32 (over x, z).
Axes of the slice: x: 4, y: 4, z: 8, core: 2. Of those that a mesh axis runs over, the one named last changes fastest.
Arguments:
- visibility: bfloat16 [2, 8, 2048, 8, 1536], P(None, 'lst', None, None, 'chan'), may hold values from -6 to 6
- inverse_cov: bfloat16 [1536, 1536], replicated, as said below
- group_size: int32 [2048], replicated, may hold values from 2 to 8, as said below
- group_owner: int32 [2048], replicated, may hold values from 0 to 2047, each once
- lst_bin: int32 [8], P('lst'), may hold values from 0 to 7
Outputs:
- power: float32 [8, 2048, 1536], P(None, 'chan', 'lst')
Inputs may be any that keep to these rules, and one draw needn't show every extreme that they name: `inverse_cov`: symmetric and positive definite. `group_size`: some group has exactly 8 live baselines; slots at or past a group's size are padding. `group_owner`: each position 0 to 2047 appears once.
All inputs are finite; a program needn't handle non-finite values.
Results may differ from a plain program's by a relative error of at most 0.0057.
Values may be sent and summed in bfloat16 or wider, within the bound.
A program may use at most 128 MiB of HBM per device.

v0:
```python
import math

import jax
import jax.numpy as jnp
from jax import lax
from jax.sharding import PartitionSpec as P

NBIN = 8


def delay_tables(channels):
    channel_index = jnp.arange(channels, dtype=jnp.int32)
    phase_index = channel_index[:, None] * channel_index[None, :] % channels
    angles = 2.0 * math.pi / channels * phase_index.astype(jnp.float32)
    base_angle = 2.0 * math.pi / channels * channel_index.astype(jnp.float32)
    window_taper = (
        0.35875
        - 0.48829 * jnp.cos(base_angle)
        + 0.14128 * jnp.cos(2.0 * base_angle)
        - 0.01168 * jnp.cos(3.0 * base_angle)
    )
    column_scale = window_taper[:, None] * (2.0 / math.sqrt(channels))
    return (
        (column_scale * jnp.cos(angles)).astype(jnp.bfloat16),
        (column_scale * jnp.sin(angles)).astype(jnp.bfloat16),
    )


def pair_power(regrouped, live_sizes, inverse_cov, tables):
    cos_table, sin_table = tables
    time_count, group_count, slot_count, channels = (
        regrouped.shape[1],
        regrouped.shape[2],
        regrouped.shape[3],
        regrouped.shape[4],
    )
    row_count = time_count * group_count * slot_count
    flat_rows = regrouped.reshape(2 * row_count, channels)
    weighted = jnp.dot(flat_rows, inverse_cov, preferred_element_type=jnp.float32).astype(
        jnp.bfloat16
    )
    joined_table = jnp.concatenate([cos_table, sin_table], axis=1)
    product = jnp.dot(weighted, joined_table, preferred_element_type=jnp.float32)
    real_cos = product[:row_count, :channels]
    real_sin = product[:row_count, channels:]
    imag_cos = product[row_count:, :channels]
    imag_sin = product[row_count:, channels:]
    grid_shape = (time_count, group_count, slot_count, channels)
    delay_real = (real_cos + imag_sin).reshape(grid_shape)
    delay_imag = (imag_cos - real_sin).reshape(grid_shape)
    live_mask = (jnp.arange(slot_count, dtype=jnp.int32)[None, :] < live_sizes[:, None]).astype(
        jnp.float32
    )[None, :, :, None]
    summed_real = jnp.sum(delay_real * live_mask, axis=2)
    summed_imag = jnp.sum(delay_imag * live_mask, axis=2)
    self_power = jnp.sum((delay_real * delay_real + delay_imag * delay_imag) * live_mask, axis=2)
    members = live_sizes.astype(jnp.float32)
    pair_count = members * (members - 1.0)
    return (summed_real * summed_real + summed_imag * summed_imag - self_power) / pair_count[
        None, :, None
    ]


def bin_power(crossed, bin_index):
    binned = []
    for which_bin in range(NBIN):
        selected = (bin_index == which_bin).astype(jnp.float32)[:, None, None]
        binned.append(jnp.sum(crossed * selected, axis=0))
    return jnp.stack(binned, axis=0)


def shards(visibility, inverse_cov, group_size, group_owner, lst_bin):
    chan_size = lax.axis_size("chan")
    group_total = group_owner.shape[0]
    held_groups = group_total // chan_size
    channels = inverse_cov.shape[0]
    owner_order = jnp.argsort(group_owner)
    tables = delay_tables(channels)
    bins_all = lax.all_gather(lst_bin, "lst", axis=0, tiled=True)
    onehot_all = (bins_all[:, None] == jnp.arange(NBIN, dtype=jnp.int32)[None, :]).astype(
        jnp.float32
    )
    counts = jnp.maximum(jnp.sum(onehot_all, axis=0), 1.0)
    column = lax.axis_index("chan")
    ordered = jnp.take(visibility, owner_order, axis=2)
    regrouped = lax.all_to_all(ordered, "chan", split_axis=2, concat_axis=4, tiled=True)
    own_groups = lax.dynamic_slice_in_dim(owner_order, column * held_groups, held_groups)
    live_sizes = jnp.take(group_size, own_groups)
    crossed = pair_power(regrouped, live_sizes, inverse_cov, tables)
    partial_value = bin_power(crossed, lst_bin)
    binned_power = (
        lax.psum_scatter(partial_value, "lst", scatter_dimension=2, tiled=True)
        / counts[:, None, None]
    )
    return binned_power


def solution(mesh):
    placed = (P(None, "lst", None, None, "chan"), P(), P(), P(), P("lst"))
    return jax.shard_map(
        shards, mesh=mesh, in_specs=placed, out_specs=P(None, "chan", "lst"), check_vma=False
    )
```

profile of v0, /device:TPU:1, one launch (start us, length us, event | category | flops | bytes accessed | tf_op | source)
XLA Modules:
  0.0 282.6 jit_solution(14444583495779701117)
XLA Ops:
  6.5 0.0 copy-start
  6.5 5.7 %sort.17 = (s32[2048]{0:T(1024)}, s32[2048]{0:T(1024)S(1)}) sort(s32[2048]{0:T(1024)} %param.8, s32[2048]{0:T(1024)S(1)} %iota.27), dimensions={0}, to_apply=%region_0.0 | sort | flops 22528 | bytes 32768 | tf_op jit(solution)/shard_map/jit(argsort)/sort | solution.py:77
  12.3 9.7 %copy.11 = bf16[2,1,2048,8,48]{4,3,2,0,1:T(8,128)(2,1)} copy(bf16[2,1,2048,8,48]{2,4,3,1,0:T(8,128)(2,1)} %param.5) | data formatting | bytes 6291456 | tf_op args[0]
  22.0 20.0 %gather_fusion = bf16[2048,2,8,48]{3,2,1,0:T(8,128)(2,1)} fusion(bf16[2,2048,8,48]{3,2,1,0:T(8,128)(2,1)} %bitcast.52, s32[2048]{0:T(1024)S(1)} %fusion.13), kind=kCustom, calls=%fused_computation | custom fusion | bytes 6299648 | tf_op jit(solution)/shard_map/jit(_take)/gather | solution.py:85
  42.1 9.4 %fusion.15 = bf16[2048,1,2,8,48]{4,3,2,1,0:T(8,128)(2,1)} fusion(bf16[2048,2,8,48]{3,2,1,0:T(8,128)(2,1)} %gather_fusion, pred[2048]{0:T(1024)(128)(4,1)S(1)} %compare_and_fusion), kind=kLoop, calls=%fused_computation.50 | loop fusion | flops 1572864 | bytes 6293504
  51.5 18.5 %reshape.549 = bf16[32,2,24576]{2,1,0:T(2,128)(2,1)} reshape(bf16[2048,1,2,8,48]{4,3,2,1,0:T(8,128)(2,1)} %fusion.15) | data formatting | bytes 6291456
  69.9 11.9 %all-to-all-start = ((bf16[32,2,24576]{2,1,0:T(2,128)(2,1)}), bf16[32,2,24576]{2,1,0:T(2,128)(2,1)S(1)}, u32[]{:S(2)}, u32[]{:S(2)}) async-start(bf16[32,2,24576]{2,1,0:T(2,128)(2,1)} %reshape.549), calls=%async_computation | async-start | bytes 6291456 | tf_op jit(solution)/shard_map/all_to_all | solution.py:86
  81.8 0.0 reduce-scatter.4.cloned.1.call-start
  82.5 0.1 compare_select_fusion.1
  82.6 0.8 gather_fusion.1
  83.4 0.1 subtract_multiply_fusion
  83.5 0.1 add_multiply_fusion
  83.6 0.1 fusion.12
  83.7 40.8 %multiply_convert_fusion.1 = (bf16[1536,1536]{1,0:T(8,128)(2,1)}, bf16[1536,1536]{1,0:T(8,128)(2,1)}) fusion(f32[1536]{0:T(1024)S(1)} %subtract_multiply_fusion), kind=kLoop, calls=%fused_computation.10 | loop fusion | flops 30670848 | bytes 9443328 | tf_op jit(solution)/shard_map/convert_element_type | solution.py:24
  124.5 28.9 %all-to-all-done = bf16[32,2,24576]{2,1,0:T(2,128)(2,1)S(1)} async-done(((bf16[32,2,24576]{2,1,0:T(2,128)(2,1)}), bf16[32,2,24576]{2,1,0:T(2,128)(2,1)S(1)}, u32[]{:S(2)}, u32[]{:S(2)}) %all-to-all-start) | async-done | bytes 3145760 | tf_op jit(solution)/shard_map/all_to_all | solution.py:86
  153.4 9.5 %reshape.550 = bf16[2048,1,2,8,48]{4,3,2,1,0:T(8,128)(2,1)} reshape(bf16[32,2,24576]{2,1,0:T(2,128)(2,1)S(1)} %all-to-all-done) | data formatting | bytes 6291456
  162.8 16.3 %copy.17 = bf16[2,1,32,64,8,48]{5,2,4,3,0,1:T(8,128)(2,1)} copy(bf16[2,1,32,64,8,48]{5,4,0,3,2,1:T(8,128)(2,1)} %bitcast.53) | data formatting | bytes 6291456 | tf_op jit(solution)/shard_map/all_to_all | solution.py:86
  179.1 14.9 %reshape.511 = bf16[1024,1536]{1,0:T(8,128)(2,1)S(1)} reshape(bf16[2,1,64,8,32,48]{5,4,3,2,0,1:T(8,128)(2,1)} %bitcast.54) | data formatting | bytes 6291456 | tf_op jit(solution)/shard_map/reshape | solution.py:38
  194.1 24.4 %fusion.2 = f32[1024,3072]{1,0:T(8,128)} fusion(bf16[1536,1536]{1,0:T(8,128)(2,1)} %get-tuple-element.15, bf16[1536,1536]{1,0:T(8,128)(2,1)} %get-tuple-element.14, bf16[1024,1536]{1,0:T(8,128)(2,1)S(1)} %reshape.511, bf16[1536,1536]{1,0:T(8,128)(2,1)} %param.6), kind=kOutput, calls=%fused_computation.5 | convolution fusion | flops 14515961856 | bytes 29884416 | tf_op jit(solution)/shard_map/dot_general | solution.py:43
  218.5 6.9 %multiply_reduce_fusion.2 = (f32[64,1536]{1,0:T(8,128)S(1)}, f32[64,1536]{1,0:T(8,128)S(1)}, f32[64,1536]{1,0:T(8,128)S(1)}) fusion(f32[64,8]{1,0:T(8,128)S(1)} %fusion.12, f32[1024,3072]{1,0:T(8,128)} %fusion.2), kind=kLoop, calls=%fused_computation.25 | loop fusion | flops 8355840 | bytes 13764608 | tf_op jit(solution)/shard_map/reduce_sum | solution.py:54
  225.4 0.1 multiply_dynamic-update-slice_fusion.7
  225.9 4.1 %copy.14 = f32[8,64,1536]{1,0,2:T(8,128)} copy(f32[8,64,1536]{2,1,0:T(8,128)S(1)} %multiply_dynamic-update-slice_fusion) | data formatting | bytes 6291456
  230.0 6.3 %reshape.547 = f32[1536,512]{1,0:T(8,128)} reshape(f32[1536,8,64]{2,1,0:T(8,128)} %bitcast.55) | data formatting | bytes 6291456
  236.3 0.0 reduce-scatter.4.cloned.1.call-update
  236.3 0.6 dynamic-slice
  236.9 0.8 dynamic-update-slice
  237.7 11.3 %all-reduce = s32[8]{0:T(128)S(1)} all-reduce(s32[8]{0:T(128)S(1)} %dynamic-update-slice), channel_id=1, replica_groups=mesh['lst'=8,'chan'=32] {'lst'}, use_global_device_ids=true, to_apply=%add | all-reduce | flops 8 | bytes 64
  248.9 0.1 convert_reduce_fusion
  249.0 24.3 %reduce-scatter.4.cloned.1.call-done = f32[192,512]{1,0:T(8,128)} async-done(((f32[1536,512]{1,0:T(8,128)}), f32[192,512]{1,0:T(8,128)}) %reduce-scatter.4.cloned.1.call-update) | async-done | bytes 393232
  273.3 1.2 reshape.548
  274.5 0.4 copy.15
  274.9 0.9 broadcast_divide_fusion
  (18 shorter events, 0.2 us)
Async XLA Ops:
  6.5 76.1 %copy-start = (s32[2048]{0:T(1024)S(1)}, s32[2048]{0:T(1024)}, u32[]{:S(2)}) copy-start(s32[2048]{0:T(1024)} %param.7) | copy-start | bytes 24580
  69.9 83.4 %all-to-all-start = ((bf16[32,2,24576]{2,1,0:T(2,128)(2,1)}), bf16[32,2,24576]{2,1,0:T(2,128)(2,1)S(1)}, u32[]{:S(2)}, u32[]{:S(2)}) async-start(bf16[32,2,24576]{2,1,0:T(2,128)(2,1)} %reshape.549), calls=%async_computation | async-start | bytes 6291456 | tf_op jit(solution)/shard_map/all_to_all | solution.py:86
  81.8 191.6 %reduce-scatter.4.cloned.1.call-start = ((), (), s32[]{:S(2)}) async-start(), calls=%async_computation.2 | async-start | bytes 3538944
  230.0 6.3 %copy-start.2 = (u32[256]{0:T(256)S(1)}, u32[256]{0:T(256)}, u32[]{:S(2)}) copy-start(u32[256]{0:T(256)} %constant.94) | copy-start | bytes 3076
  230.0 45.8 %copy-start.1 = (s32[2048]{0:T(1024)S(1)}, s32[2048]{0:T(1024)}, u32[]{:S(2)}) copy-start(s32[2048]{0:T(1024)} %param.7) | copy-start | bytes 24580
Sparse Core Ops, SparseCore 0:
  236.4 36.8 reduce-scatter.3
where the time goes:
time: 285 us; the launch traced here: 283 us
  local copies, waits for them, and re-layouts  103 us (36%)
  other arithmetic  64.6 us (23%)
  waiting for transfers between devices  53.2 us (19%)
  matrix products  24.4 us (9%)
  between operations  14.2 us (5%)
  starting transfers between devices  11.9 us (4%)
  blocking collectives  11.3 us (4%)
    unnamed x16, local copies, waits for them, and re-layouts  50.9 us
    convert_element_type x1, other arithmetic, delay_tables(): (column_scale * jnp.cos(angles)).astype(jnp.bfloat16)  40.8 us
    all_to_all x1, waiting for transfers between devices, shards(): lax.all_to_all(ordered, 'chan', split_axis=2, concat_axis=4, tiled=True)  28.9 us
    dot_general x1, matrix products, pair_power(): jnp.dot(weighted, joined_table, preferred_element_type=jnp.float32)  24.4 us
    unnamed x2, waiting for transfers between devices  24.3 us
    gather x1, local copies, waits for them, and re-layouts, shards(): ordered = jnp.take(visibility, owner_order, axis=2)  20 us
    all_to_all x1, local copies, waits for them, and re-layouts, shards(): lax.all_to_all(ordered, 'chan', split_axis=2, concat_axis=4, tiled=True)  16.3 us
    reshape x1, local copies, waits for them, and re-layouts, pair_power(): flat_rows = regrouped.reshape(2 * row_count, channels)  14.9 us
  transfers between devices with their start and end apart: 2, of which 2 were waited for; matrix products, arithmetic and copies ran while one was open for 15% of the time, Pallas kernels for 0%

commit v1 on v0

v1 whole, which is shorter than its diff:
```python
import functools
import math

import jax
import jax.numpy as jnp
from jax import lax
from jax.experimental import pallas as pl
from jax.experimental.pallas import tpu as pltpu
from jax.sharding import PartitionSpec as P

NBIN = 8
SLOT = 8
MESH = pl.DeviceIdType.MESH
F32 = jnp.float32
BF16 = jnp.bfloat16
NN = (((1,), (0,)), ((), ()))
NT = (((1,), (1,)), ((), ()))
TN = (((0,), (0,)), ((), ()))
ORDER = ((4, 3, 5, 0), (2, 6, 1, 7))
TAIL = 16


def dot(a, b, dims=NN):
    return lax.dot_general(a, b, dims, preferred_element_type=F32)


def one_if(condition):
    return jnp.where(condition, 1.0, 0.0).astype(BF16)


def kernel(
    cap,
    sizes,
    bin_ref,
    owner_ref,
    size_ref,
    vis_ref,
    cov_hbm,
    out_ref,
    cov,
    gathered,
    paired,
    send,
    rows,
    table,
    fold,
    acc,
    step_cos,
    step_sin,
    base_cos,
    base_sin,
    member,
    plus,
    minus,
    landed,
    bin_send,
    bin_land,
    cov_sem,
    own_sem,
    send_sem,
    recv_sem,
    y_send,
    y_recv,
    b_send,
    b_recv,
):
    nx, nz, nl, held, channels, width = sizes
    half = channels // 2
    part = channels // nl
    lst = lax.axis_index("lst")
    chan = lax.axis_index("chan")
    x, z = chan // nz, chan % nz
    quads = nx * nz // 4
    per_x = nz // 4

    def place(q, i):
        dz = ORDER[0][i] + (q % per_x) * (ORDER[1][i] - ORDER[0][i])
        return lax.rem(x + q // per_x, nx) * nz + lax.rem(z + dz, nz)

    def landing():
        return rows.at[pl.ds(pl.multiple_of(chan * width, 16), width), :]

    def block_copy(q, i):
        n = 4 * q + i
        return pltpu.make_async_remote_copy(
            src_ref=send.at[n],
            dst_ref=landing(),
            send_sem=send_sem.at[n],
            recv_sem=recv_sem.at[n],
            device_id=(lst, place(q, i)),
            device_id_type=MESH,
        )

    own_copy = pltpu.make_async_copy(send.at[3], landing(), own_sem)
    cov_copy = pltpu.make_async_copy(cov_hbm, cov, cov_sem)

    barrier = pltpu.get_barrier_semaphore()
    for other in range(1, nx * nz):
        peer = lax.rem(x + other // nz, nx) * nz + lax.rem(z + other % nz, nz)
        pl.semaphore_signal(barrier, inc=1, device_id=(lst, peer), device_id_type=MESH)
    for dl in range(1, nl):
        pl.semaphore_signal(
            barrier, inc=1, device_id=(lax.rem(lst + dl, nl), chan), device_id_type=MESH
        )
    cov_copy.start()
    bin_send[...] = jnp.full(bin_send.shape, bin_ref[0], jnp.int32).astype(F32).astype(BF16)
    plus[pl.ds(half, TAIL), :] = jnp.zeros((TAIL, held), BF16)

    low = lax.broadcasted_iota(jnp.int32, (width, 2 * held), 1) < held
    rank = lax.broadcasted_iota(jnp.int32, (held, cap), 1)
    spot = lax.broadcasted_iota(jnp.int32, (4 * held, 1), 0)

    def quad(q, first):
        base = jnp.zeros((4 * held, 1), jnp.int32)
        for i in range(4):
            here = (spot >= i * held) & (spot < (i + 1) * held)
            base = jnp.where(here, place(q, i) * held - i * held, base)
        hit = owner_ref[...] == base + spot
        live = jnp.sum(jnp.where(hit, size_ref[...], 0), axis=1, keepdims=True)
        row_id = lax.broadcasted_iota(jnp.int32, (4 * held, 4 * held), 0)
        col_id = lax.broadcasted_iota(jnp.int32, (4 * held, 4 * held), 1)
        before = one_if((row_id // held == col_id // held) & (col_id < row_id))
        live_wide = jnp.broadcast_to(live.astype(F32), (4 * held, 128)).astype(BF16)
        start = dot(before, live_wide)[:, :1].astype(jnp.int32)
        gathered[...] = dot(vis_ref[...], one_if(hit), NT)
        for i in range(4):
            for c in range(2):
                for pair in range(SLOT // 2):
                    r0 = (c * SLOT + 2 * pair) * width
                    lanes = pl.ds((i // 2) * 2 * held, 2 * held)
                    left = gathered[pl.ds(r0, width), lanes]
                    right = gathered[pl.ds(r0 + width, width), lanes]
                    if i % 2 == 0:
                        joined = jnp.where(low, left, pltpu.roll(right, held, 1))
                    else:
                        joined = jnp.where(low, pltpu.roll(left, held, 1), right)
                    paired[i, pl.ds(c * width, width), pl.ds(pair * 2 * held, 2 * held)] = (
                        joined.astype(BF16)
                    )
        for i in range(4):
            live_i = live[i * held : (i + 1) * held]
            start_i = start[i * held : (i + 1) * held]
            chosen = [
                one_if(rank == jnp.where(live_i > s, start_i + s, -1)) for s in range(SLOT)
            ]
            block = dot(paired[i], jnp.concatenate(chosen, axis=0)).astype(BF16)
            send[4 * q + i, :, pl.ds(0, cap)] = block[:width]
            send[4 * q + i, :, pl.ds(cap, cap)] = block[width:]
            if i > 0:
                if first and i == 1:
                    pl.semaphore_wait(barrier, nx * nz - 1 + nl - 1)
                block_copy(q, i - 1).start()
            elif not first:

                @pl.when(q > 1)
                def _():
                    block_copy(q - 1, 3).start()

                @pl.when(q == 1)
                def _():
                    own_copy.start()

            if first and i == 3:
                member[...] = one_if((rank >= start_i) & (rank < start_i + live_i))

    quad(0, True)

    def later(q, carry):
        quad(q, False)
        return carry

    lax.fori_loop(1, quads, later, 0)
    block_copy(quads - 1, 3).start()

    def bin_copy(dl):
        return pltpu.make_async_remote_copy(
            src_ref=bin_send,
            dst_ref=bin_land.at[lst],
            send_sem=b_send.at[dl],
            recv_sem=b_recv.at[dl],
            device_id=(lax.rem(lst + dl, nl), chan),
            device_id_type=MESH,
        )

    for dl in range(1, nl):
        bin_copy(dl).start()
    bin_land[lst] = bin_send[...]

    steps = step_cos.shape[0]
    bases = half // steps
    unit = 2.0 * math.pi / channels

    def phase(k, f):
        product = k * f
        turns = jnp.floor(product * (1.0 / channels))
        return (product - turns * channels) * unit

    def grid(shape, dim):
        return lax.broadcasted_iota(jnp.int32, shape, dim).astype(F32)

    shape = (steps, channels)
    angle = phase(grid(shape, 0), grid(shape, 1))
    step_cos[...] = jnp.cos(angle)
    step_sin[...] = jnp.sin(angle)
    shape = (base_cos.shape[0], channels)
    angle = grid(shape, 1) * unit
    taper = (
        0.35875
        - 0.48829 * jnp.cos(angle)
        + 0.14128 * jnp.cos(2.0 * angle)
        - 0.01168 * jnp.cos(3.0 * angle)
    ) * (2.0 / math.sqrt(channels))
    angle = phase(grid(shape, 0) * float(steps), grid(shape, 1))
    base_cos[...] = taper * jnp.cos(angle)
    base_sin[...] = taper * jnp.sin(angle)
    channel = lax.broadcasted_iota(jnp.int32, (1, channels), 1)
    middle = taper[:1] * jnp.where(channel % 2 == 0, 1.0, -1.0)
    step_row = lax.broadcasted_iota(jnp.int32, (steps, channels), 0)

    def tables(a, carry):
        bc, bs = base_cos[pl.ds(a, 1), :], base_sin[pl.ds(a, 1), :]
        uc, us = step_cos[...], step_sin[...]
        at = pl.multiple_of(a * steps, steps)
        table[pl.ds(at, steps), :] = (uc * bc - us * bs).astype(BF16)
        sines = jnp.where(step_row + at == 0, middle, us * bc + uc * bs)
        table[pl.ds(half + at, steps), :] = sines.astype(BF16)
        return carry

    lax.fori_loop(0, bases, tables, 0)
    cov_copy.wait()
    tall = 256

    def folding(i, carry):
        at = pl.ds(pl.multiple_of(i * tall, tall), tall)
        fold[at, :] = dot(table[at, :], cov[...]).astype(BF16)
        return carry

    lax.fori_loop(0, channels // tall, folding, 0)
    own_copy.wait()

    def arrive(q):
        for i in range(4):

            @pl.when(4 * q + i != 3)
            def _():
                block_copy(q, i).wait_recv()

    deep = nz * width

    def group(g, carry):
        for odd in range(per_x):
            arrive(per_x * g + odd)
        from_x = lax.rem(x + nx - g, nx)
        ch = pl.ds(pl.multiple_of(from_x * deep, deep), deep)

        def strip(i, inner):
            at = pl.ds(pl.multiple_of(i * tall, tall), tall)
            part_sum = dot(fold[at, ch], rows[ch, :])

            @pl.when(g == 0)
            def _():
                acc[at, :] = part_sum

            @pl.when(g > 0)
            def _():
                acc[at, :] += part_sum

            return inner

        return lax.fori_loop(0, channels // tall, strip, carry)

    lax.fori_loop(0, nx, group, 0)

    members = dot(jnp.ones((8, cap), BF16), member[...], NT)[:1]
    scale = 1.0 / (members * (members - 1.0))

    def share_copy(source, h, to, dl):
        return pltpu.make_async_remote_copy(
            src_ref=source.at[pl.ds(pl.multiple_of(h * part, 16), part + TAIL), :],
            dst_ref=landed.at[lst],
            send_sem=y_send.at[to],
            recv_sem=y_recv.at[dl],
            device_id=(to, chan),
            device_id_type=MESH,
        )

    def share(source, h, to):
        @pl.when(to != lst)
        def _():
            share_copy(source, h, to, lax.rem(to - lst + nl, nl)).start()

        @pl.when(to == lst)
        def _():
            landed[lst] = source[pl.ds(pl.multiple_of(h * part, 16), part + TAIL), :]

    def finish(h, carry):
        at = pl.multiple_of(h * part, part)
        rc = acc[pl.ds(at, part), pl.ds(0, cap)]
        ic = acc[pl.ds(at, part), pl.ds(cap, cap)]
        rs = acc[pl.ds(half + at, part), pl.ds(0, cap)]
        im = acc[pl.ds(half + at, part), pl.ds(cap, cap)]
        ends = lax.broadcasted_iota(jnp.int32, (part, 1), 0) + at == 0
        even = rc * rc + ic * ic
        odd = rs * rs + im * im
        cross = 2.0 * (rc * im - ic * rs)
        power_plus = jnp.where(ends, even, even + odd + cross).astype(BF16)
        power_minus = jnp.where(ends, odd, even + odd - cross).astype(BF16)
        mine = member[...]

        def total(v):
            return dot(v, mine, NT)

        def exact(v):
            head = v.astype(BF16)
            return total(head) + total((v - head.astype(F32)).astype(BF16))

        src, sic = exact(rc), exact(ic)
        srs, sim = exact(rs), exact(im)
        zero = jnp.zeros_like(src)
        a, b = jnp.where(ends, src, src + sim), jnp.where(ends, sic, sic - srs)
        plus[pl.ds(at, part), :] = ((a * a + b * b - total(power_plus)) * scale).astype(BF16)
        a, b = jnp.where(ends, srs, src - sim), jnp.where(ends, sim, sic + srs)
        under = ((a * a + b * b - total(power_minus)) * scale).astype(BF16)
        minus[pl.ds(at, part), :] = under

        @pl.when(h == 0)
        def _():
            minus[pl.ds(half, TAIL), :] = under[:TAIL]

        @pl.when(h > 0)
        def _():
            share(plus, h - 1, h - 1)
            share(minus, h - 1, nl - h)

        return carry

    spans = half // part
    lax.fori_loop(0, spans, finish, 0)
    share(plus, spans - 1, spans - 1)
    share(minus, spans - 1, nl - spans)

    for dl in range(1, nl):
        bin_copy(dl).wait()
        share_copy(plus, 0, lax.rem(lst + dl, nl), dl).wait_recv()
    row = lax.broadcasted_iota(jnp.int32, (part + TAIL, part), 0)
    col = lax.broadcasted_iota(jnp.int32, (part + TAIL, part), 1)
    turn = one_if(row == jnp.where(lst < spans, col, part - col))
    for t in range(nl):
        piece = dot(landed[t], turn, TN)
        code = bin_land[t].astype(F32)[:1, :1]
        for b in range(NBIN):
            term = jnp.where(code == b, piece, 0.0)
            if t == 0:
                out_ref[b] = term
            else:
                out_ref[b] += term
    for b in range(NBIN):
        count = jnp.zeros((1, 1), F32)
        for t in range(nl):
            count += jnp.where(bin_land[t].astype(F32)[:1, :1] == b, 1.0, 0.0)
        out_ref[b] = out_ref[b] / jnp.maximum(count, 1.0)

    def sent(q, carry):
        for i in range(4):

            @pl.when(4 * q + i != 3)
            def _():
                block_copy(q, i).wait_send()

        return carry

    lax.fori_loop(0, quads, sent, 0)
    for dl in range(1, nl):
        to = lax.rem(lst + dl, nl)
        share_copy(plus, 0, to, dl).wait_send()


def cross_power(cap, collective_id, sizes, lst_bin, owner, size, vis, cov):
    nx, nz, nl, held, channels, width = sizes
    half = channels // 2
    part = channels // nl
    total = nx * nz
    vmem = pltpu.VMEM
    dma = pltpu.SemaphoreType.DMA
    return pl.pallas_call(
        functools.partial(kernel, cap, sizes),
        out_shape=jax.ShapeDtypeStruct((NBIN, held, part), F32),
        in_specs=[
            pl.BlockSpec(memory_space=pltpu.SMEM),
            pl.BlockSpec(memory_space=vmem),
            pl.BlockSpec(memory_space=vmem),
            pl.BlockSpec(memory_space=vmem),
            pl.BlockSpec(memory_space=pl.ANY),
        ],
        out_specs=pl.BlockSpec(memory_space=vmem),
        scratch_shapes=[
            vmem((channels, channels), BF16),
            vmem((2 * SLOT * width, 4 * held), F32),
            vmem((4, 2 * width, SLOT * held), BF16),
            vmem((total, width, 2 * cap), BF16),
            vmem((channels, 2 * cap), BF16),
            vmem((channels, channels), BF16),
            vmem((channels, channels), BF16),
            vmem((channels, 2 * cap), F32),
            vmem((64, channels), F32),
            vmem((64, channels), F32),
            vmem((16, channels), F32),
            vmem((16, channels), F32),
            vmem((held, cap), BF16),
            vmem((half + TAIL, held), BF16),
            vmem((half + TAIL, held), BF16),
            vmem((nl, part + TAIL, held), BF16),
            vmem((16, 128), BF16),
            vmem((nl, 16, 128), BF16),
            dma(()),
            dma(()),
            dma((total,)),
            dma((total,)),
            dma((nl,)),
            dma((nl,)),
            dma((nl,)),
            dma((nl,)),
        ],
        compiler_params=pltpu.CompilerParams(
            collective_id=collective_id, has_side_effects=True, vmem_limit_bytes=60 * 2**20
        ),
    )(lst_bin, owner, size, vis, cov)


def solution(mesh):
    nl, total = mesh.shape["lst"], mesh.shape["chan"]
    nx = total // 8
    nz = total // nx

    def shards(visibility, inverse_cov, group_size, group_owner, lst_bin):
        groups, width = visibility.shape[2], visibility.shape[4]
        channels = inverse_cov.shape[0]
        held = groups // total
        sizes = (nx, nz, nl, held, channels, width)
        vis = jnp.transpose(visibility, (0, 1, 3, 4, 2)).reshape(2 * SLOT * width, groups)
        owner = group_owner.reshape(1, groups)
        size = group_size.reshape(1, groups)
        home = group_owner[None, :] // held == jnp.arange(total, dtype=jnp.int32)[:, None]
        most = jnp.max(jnp.sum(jnp.where(home, size, 0), axis=1))
        full = SLOT * held
        tight = full * 3 // 4
        return lax.cond(
            most <= tight,
            functools.partial(cross_power, tight, 0, sizes),
            functools.partial(cross_power, full, 1, sizes),
            lst_bin, owner, size, vis, inverse_cov,
        )

    placed = (P(None, "lst", None, None, "chan"), P(), P(), P(), P("lst"))
    return jax.shard_map(
        shards, mesh=mesh, in_specs=placed, out_specs=P(None, "chan", "lst"), check_vma=False
    )
```

time: 285 us -> 84.3 us (0.30)
  local copies, waits for them, and re-layouts: 103 us -> 0.8 us
  Pallas kernels: 0 us -> 80 us
  other arithmetic: 64.6 us -> 2.18 us
  waiting for transfers between devices: 53.2 us -> 0 us
  matrix products: 24.4 us -> 0 us
  between operations: 14.2 us -> 0.66 us
  starting transfers between devices: 11.9 us -> 0 us
  blocking collectives: 11.3 us -> 0 us
    pallas_call x0 -> x1, Pallas kernels: none -> 80 us  [cross_power(): pl.pallas_call(functools.partial(kernel, cap, sizes), out_shape=jax.Shape...]
    unnamed x16 -> x1, local copies, waits for them, and re-layouts: 50.9 us -> 0.8 us
    convert_element_type x2 -> x0, other arithmetic: 40.9 us -> none  [the longest x1 40.8 us: delay_tables(): (column_scale * jnp.cos(angles)).astype(jnp.bfloat16)]
    all_to_all x1 -> x0, waiting for transfers between devices: 28.9 us -> none  [shards(): lax.all_to_all(ordered, 'chan', split_axis=2, concat_axis=4, tiled=True)]
    dot_general x1 -> x0, matrix products: 24.4 us -> none  [pair_power(): jnp.dot(weighted, joined_table, preferred_element_type=jnp.float32)]
    unnamed x2 -> x0, waiting for transfers between devices: 24.3 us -> none
    gather x2 -> x0, local copies, waits for them, and re-layouts: 20.8 us -> none  [the longest x1 20 us: shards(): ordered = jnp.take(visibility, owner_order, axis=2)]
    all_to_all x1 -> x0, local copies, waits for them, and re-layouts: 16.3 us -> none  [shards(): lax.all_to_all(ordered, 'chan', split_axis=2, concat_axis=4, tiled=True)]
  transfers between devices with their start and end apart: 2 -> 0, of which waited for: 2 -> 0; matrix products, arithmetic and copies ran while one was open for 15% -> 0% of each run, Pallas kernels for 0% -> 0%
where the time goes in v1:
time: 84.3 us; the launch traced here: 84.1 us
  Pallas kernels  80 us (95%)
  other arithmetic  2.18 us (3%)
    pallas_call x1, Pallas kernels, cross_power(): pl.pallas_call(functools.partial(kernel, cap, sizes), out_shape=jax.Shape...  80 us

profile of v1, /device:TPU:1, one launch (start us, length us, event | category | flops | bytes accessed | tf_op | source)
XLA Modules:
  0.0 84.1 jit_solution(4150022912131797980)
XLA Ops:
  0.0 0.7 add_select_fusion
  0.7 0.8 select_reduce_fusion
  1.5 0.6 reduce_max.9
  2.8 80.4 %conditional.1 = (f32[8,64,192]{2,1,0:T(8,128)S(1)}) conditional(s32[]{:T(128)} %convert_element_type.3, (s32[1]{0:T(128)}, s32[2048]{0:T(1024)}, s32[2048]{0:T(1024)}, bf16[2,1,8,48,2048]{4,3,2,0,1:T(8,128)(2,1)}, bf16[1536,1536]{1,0:T(8,128)(2,1)}) %tuple.16, (s32[1]{0:T(128)}, s32[2048]{0:T(1024)}, s32[2048]{0:T(1024)}, ...), branch_computations={%region_2.3_spmd, %region_3.4_spmd} | conditional | bytes 8 | solution.py:447
  3.0 80.0 %branch_1_fun.1 = f32[8,64,192]{2,1,0:T(8,128)S(1)} custom-call(s32[1]{0:T(128)} %get-tuple-element.50.bin_ref, s32[1,2048]{1,0:T(1,128)} %bitcast.16, s32[1,2048]{1,0:T(1,128)} %bitcast.14, bf16[768,2048]{1,0:T(8,128)(2,1)} %bitcast.12, bf16[1536,1536]{1,0:T(8,128)(2,1)} %get-tuple-element.52.cov_hbm), custom_call_target="tpu_custom_call" | custom-call | tf_op jit(solution)/shard_map/cond/branch_1_fun/pallas_call | solution.py:385
  83.3 0.8 copy.17

commit v2 on v1

v2 whole, which is shorter than its diff:
```python
import functools
import math

import jax
import jax.numpy as jnp
from jax import lax
from jax.experimental import pallas as pl
from jax.experimental.pallas import tpu as pltpu
from jax.sharding import PartitionSpec as P

NBIN = 8
SLOT = 8
MESH = pl.DeviceIdType.MESH
F32 = jnp.float32
BF16 = jnp.bfloat16
NN = (((1,), (0,)), ((), ()))
NT = (((1,), (1,)), ((), ()))
TN = (((0,), (0,)), ((), ()))
TAIL = 16
LANES = 128


def dot(a, b, dims=NN):
    return lax.dot_general(a, b, dims, preferred_element_type=F32)


def one_if(condition):
    return jnp.where(condition, 1.0, 0.0).astype(BF16)


def fits_kernel(base, room, sizes, owner_ref, size_ref, out_ref):
    nx, nz, nl, held, channels, width = sizes
    first = lax.broadcasted_iota(jnp.int32, (nx * nz, 1), 0) * held
    owner = owner_ref[...]
    mine = (owner >= first) & (owner < first + held)
    lives = jnp.sum(jnp.where(mine, size_ref[...], 0), axis=1, keepdims=True)
    over = jnp.maximum(lives - base, 0).reshape(nx, nz, 1)
    out_ref[0] = jnp.where(jnp.max(jnp.sum(over, axis=0)) <= room, 1, 0)


def kernel(
    cap,
    sizes,
    bin_ref,
    owner_ref,
    size_ref,
    vis_ref,
    cov_hbm,
    out_ref,
    cov,
    pick,
    chosen,
    gathered,
    paired,
    send_a,
    send_b,
    send_p,
    rows_a,
    rows_b,
    rows_p,
    table,
    fold,
    step_cos,
    step_sin,
    base_cos,
    base_sin,
    member_a,
    member_b,
    member_p,
    scale_ref,
    sums,
    share_plus,
    share_minus,
    landed,
    pieces,
    bin_send,
    bin_land,
    cov_sem,
    own_sem,
    a_send,
    a_recv,
    b_send,
    b_recv,
    p_send,
    p_recv,
    f_send,
    f_recv,
    y_send,
    y_recv,
    n_send,
    n_recv,
):
    nx, nz, nl, held, channels, width = sizes
    half = channels // 2
    part = channels // nl
    spans = half // part
    base = cap + held
    wide = cap + 2 * LANES
    lst = lax.axis_index("lst")
    chan = lax.axis_index("chan")
    x, z = chan // nz, chan % nz
    last = nz - 1

    def ahead(q):
        return nz // 2 + (1 - 2 * (q % 2)) * ((q + 1) // 2)

    def place(q, i):
        return lax.rem(x + i, nx) * nz + lax.rem(z + ahead(q), nz)

    def rows_of(ref, source):
        return ref.at[pl.ds(pl.multiple_of(source * width, 16), width), :]

    def a_copy(q, i):
        n = nx * q + i
        return pltpu.make_async_remote_copy(
            src_ref=send_a.at[n],
            dst_ref=rows_of(rows_a, chan),
            send_sem=a_send.at[n],
            recv_sem=a_recv.at[n],
            device_id=(lst, place(q, i)),
            device_id_type=MESH,
        )

    def b_copy(q, i):
        n = nx * q + i
        return pltpu.make_async_remote_copy(
            src_ref=send_b.at[n],
            dst_ref=rows_of(rows_b, chan),
            send_sem=b_send.at[n],
            recv_sem=b_recv.at[n],
            device_id=(lst, place(q, i)),
            device_id_type=MESH,
        )

    def p_copy(q):
        return pltpu.make_async_remote_copy(
            src_ref=send_p.at[q],
            dst_ref=rows_of(rows_p, chan),
            send_sem=p_send.at[q],
            recv_sem=p_recv.at[q],
            device_id=(lst, place(q, 0)),
            device_id_type=MESH,
        )

    def f_copy(q, j):
        source = x * nz + lax.rem(z + nz - ahead(q), nz)
        n = (nx - 1) * q + j - 1
        return pltpu.make_async_remote_copy(
            src_ref=rows_of(rows_p, source),
            dst_ref=rows_of(rows_p, source),
            send_sem=f_send.at[n],
            recv_sem=f_recv.at[n],
            device_id=(lst, lax.rem(x + j, nx) * nz + z),
            device_id_type=MESH,
        )

    own_a = pltpu.make_async_copy(send_a.at[nx * last], rows_of(rows_a, chan), own_sem.at[0])
    own_b = pltpu.make_async_copy(send_b.at[nx * last], rows_of(rows_b, chan), own_sem.at[1])
    own_p = pltpu.make_async_copy(send_p.at[last], rows_of(rows_p, chan), own_sem.at[2])
    cov_copy = pltpu.make_async_copy(cov_hbm, cov, cov_sem)

    barrier = pltpu.get_barrier_semaphore()
    for other in range(1, nx * nz):
        peer = lax.rem(x + other // nz, nx) * nz + lax.rem(z + other % nz, nz)
        pl.semaphore_signal(barrier, inc=1, device_id=(lst, peer), device_id_type=MESH)
    for dl in range(1, nl):
        pl.semaphore_signal(
            barrier, inc=1, device_id=(lax.rem(lst + dl, nl), chan), device_id_type=MESH
        )
    cov_copy.start()

    low = lax.broadcasted_iota(jnp.int32, (width, LANES), 1) < held
    lane = lax.broadcasted_iota(jnp.int32, (1, wide), 1)
    spot = lax.broadcasted_iota(jnp.int32, (held, LANES), 0).astype(F32).astype(BF16)
    row_id = lax.broadcasted_iota(jnp.int32, (nx * held, nx * held), 0)
    col_id = lax.broadcasted_iota(jnp.int32, (nx * held, nx * held), 1)
    before = one_if((row_id // held == col_id // held) & (col_id < row_id))
    one, none = jnp.ones((held, LANES), BF16), jnp.zeros((held, LANES), BF16)

    def members(start, live, pooled):
        at = lax.broadcasted_iota(jnp.int32, (held, cap), 1)
        mine = one_if((at >= start) & (at < start + live))
        empty = jnp.zeros((held, cap), BF16)
        member_a[pl.ds(0, held), :] = jnp.concatenate([mine, empty], axis=1)
        member_a[pl.ds(held, held), :] = jnp.concatenate([empty, mine], axis=1)
        at = lax.broadcasted_iota(jnp.int32, (held, LANES), 1)
        below = at < held
        near = lax.rem(at, held) + cap
        mine = (near >= start) & (near < start + live)
        member_b[pl.ds(0, held), :] = one_if(mine & below)
        member_b[pl.ds(held, held), :] = one_if(mine & jnp.logical_not(below))
        far = at + base - pooled
        mine = one_if((far >= jnp.maximum(start, base)) & (far < start + live))
        empty = jnp.zeros((held, LANES), BF16)
        member_p[pl.ds(0, held), :] = jnp.concatenate([mine, empty], axis=1)
        member_p[pl.ds(held, held), :] = jnp.concatenate([empty, mine], axis=1)
        row_id = lax.broadcasted_iota(jnp.int32, (held, LANES), 0)
        lane = lax.rem(lax.broadcasted_iota(jnp.int32, (held, LANES), 1), held)
        spread = jnp.where(row_id == lane, jnp.broadcast_to(live, (held, LANES)), 0)
        count = jnp.sum(spread.astype(F32), axis=0, keepdims=True)
        scale_ref[...] = jnp.broadcast_to(1.0 / (count * (count - 1.0)), scale_ref.shape)

    def column(q, first):
        groups = owner_ref.shape[1]
        lives = []
        for i in range(nx):
            seat = owner_ref[...] - place(q, i) * held
            seat = jnp.where((seat >= 0) & (seat < held), seat, -1).astype(F32).astype(BF16)
            sized = size_ref[...].astype(F32).astype(BF16)
            live_sum = none
            for g in range(0, groups, LANES):
                hit = jnp.broadcast_to(seat[:, g : g + LANES], (held, LANES)) == spot
                pick[pl.ds(i * held, held), pl.ds(g, LANES)] = jnp.where(hit, one, none)
                sizes_here = jnp.broadcast_to(sized[:, g : g + LANES], (held, LANES))
                live_sum += jnp.where(hit, sizes_here, none)
            lives.append(jnp.sum(live_sum.astype(F32), axis=1, keepdims=True))
        live = jnp.concatenate(lives, axis=0)
        live_wide = jnp.broadcast_to(live, (nx * held, LANES)).astype(BF16)
        start = dot(before, live_wide)[:, :1].astype(jnp.int32)
        live = live.astype(jnp.int32)
        gathered[...] = dot(vis_ref[...], pick[...], NT)
        for i in range(nx):
            for c in range(2):
                for pair in range(SLOT // 2):
                    r0 = (c * SLOT + 2 * pair) * width
                    lanes = pl.ds((i // 2) * LANES, LANES)
                    left = gathered[pl.ds(r0, width), lanes]
                    right = gathered[pl.ds(r0 + width, width), lanes]
                    if i % 2 == 0:
                        joined = jnp.where(low, left, pltpu.roll(right, held, 1))
                    else:
                        joined = jnp.where(low, pltpu.roll(left, held, 1), right)
                    paired[i, pl.ds(c * width, width), pl.ds(pair * LANES, LANES)] = (
                        joined.astype(BF16)
                    )
        ends = (start + live).reshape(nx, held, 1)
        over = [jnp.maximum(ends[i, held - 1 : held] - base, 0) for i in range(nx)]
        pool = None
        for i in range(nx):
            pooled = jnp.zeros((1, 1), jnp.int32)
            for j in range(nx):
                if j != i:
                    ahead_of = lax.rem(x + j, nx) < lax.rem(x + i, nx)
                    pooled += jnp.where(ahead_of, over[j], 0)
            live_i = live[i * held : (i + 1) * held]
            start_i = start[i * held : (i + 1) * held]
            far = lane - (cap + LANES)
            far = jnp.where(far >= pooled, far - pooled + base, -1)
            rank = jnp.where(lane < cap + LANES, jnp.where(lane < base, lane, -1), far)
            slot = rank - start_i
            slot = jnp.where((slot < live_i) & (rank >= 0), slot, -1).astype(F32).astype(BF16)
            for s in range(SLOT):
                chosen[pl.ds(s * held, held), :] = jnp.where(
                    slot == float(s), jnp.ones_like(slot), jnp.zeros_like(slot)
                )
            block = dot(paired[i], chosen[...])
            n = nx * q + i
            send_a[n, :, pl.ds(0, cap)] = block[:width, :cap].astype(BF16)
            send_a[n, :, pl.ds(cap, cap)] = block[width:, :cap].astype(BF16)
            re, im = block[:width, cap : cap + LANES], block[width:, cap : cap + LANES]
            send_b[n] = jnp.where(low, re, pltpu.roll(im, held, 1)).astype(BF16)
            extra = block[:, cap + LANES :]
            pool = extra if pool is None else pool + extra
            if first:
                if i == 1:
                    pl.semaphore_wait(barrier, nx * nz - 1 + nl - 1)
                if i > 0:
                    a_copy(q, i - 1).start()
            elif i == 0:
                a_copy(q - 1, nx - 1).start()
                p_copy(q - 1).start()

                @pl.when(q == last)
                def _():
                    members(start_i, live_i, pooled)

            elif i == 1:

                @pl.when(q < last)
                def _():
                    a_copy(q, 0).start()

                @pl.when(q == last)
                def _():
                    own_a.start()
                    own_b.start()

            else:
                a_copy(q, i - 1).start()
        send_p[q, :, pl.ds(0, LANES)] = pool[:width].astype(BF16)
        send_p[q, :, pl.ds(LANES, LANES)] = pool[width:].astype(BF16)

    column(0, True)

    def later(q, carry):
        column(q, False)
        return carry

    lax.fori_loop(1, nz, later, 0)
    bin_send[...] = jnp.full(bin_send.shape, bin_ref[0], jnp.int32).astype(F32).astype(BF16)
    a_copy(last, nx - 1).start()
    own_p.start()

    def others(each):
        def some(q, carry):
            for i in range(nx):
                if i > 0:
                    each(q, i)
                else:

                    @pl.when(q < last)
                    def _():
                        each(q, 0)

            return carry

        lax.fori_loop(0, nz, some, 0)

    others(lambda q, i: b_copy(q, i).start())

    def bin_copy(dl):
        return pltpu.make_async_remote_copy(
            src_ref=bin_send,
            dst_ref=bin_land.at[lst],
            send_sem=n_send.at[dl],
            recv_sem=n_recv.at[dl],
            device_id=(lax.rem(lst + dl, nl), chan),
            device_id_type=MESH,
        )

    for dl in range(1, nl):
        bin_copy(dl).start()
    bin_land[lst] = bin_send[...]

    steps = step_cos.shape[0]
    bases = half // steps
    unit = 2.0 * math.pi / channels
    shape = (16, channels)
    bit = lax.broadcasted_iota(jnp.int32, shape, 0)
    f = lax.broadcasted_iota(jnp.int32, shape, 1).astype(F32)
    power = jnp.zeros(shape, F32)
    for n in range(10):
        power = jnp.where(bit == n, float(2**n), power)
    product = power * f
    angle = (product - jnp.floor(product * (1.0 / channels)) * channels) * unit
    bit_cos, bit_sin = jnp.cos(angle), jnp.sin(angle)
    shape = (8, channels)
    within = lax.broadcasted_iota(jnp.int32, shape, 0)

    def turned_by(v, n):
        c, s = bit_cos[n : n + 1], bit_sin[n : n + 1]
        return v[0] * c - v[1] * s, v[1] * c + v[0] * s

    def eight(low_bit, v):
        for n in range(3):
            w = turned_by(v, low_bit + n)
            on = (within // 2**n) % 2 == 1
            v = tuple(jnp.where(on, new, old) for new, old in zip(w, v))
        return v

    tiles = [eight(0, (jnp.ones(shape, F32), jnp.zeros(shape, F32)))]
    for n in range(3, 6):
        tiles += [turned_by(v, n) for v in tiles]
    for n, v in enumerate(tiles):
        step_cos[pl.ds(8 * n, 8), :], step_sin[pl.ds(8 * n, 8), :] = v
    f = f[:8] * unit
    taper = (
        0.35875
        - 0.48829 * bit_cos[:1]
        + 0.14128 * bit_cos[1:2]
        - 0.01168 * jnp.cos(3.0 * f)[:1]
    ) * (2.0 / math.sqrt(channels))
    v = eight(6, (jnp.broadcast_to(taper, shape), jnp.zeros(shape, F32)))
    base_cos[pl.ds(0, 8), :], base_sin[pl.ds(0, 8), :] = v
    base_cos[pl.ds(8, 8), :], base_sin[pl.ds(8, 8), :] = turned_by(v, 9)
    channel = lax.broadcasted_iota(jnp.int32, (1, channels), 1)
    middle = taper * jnp.where(channel % 2 == 0, 1.0, -1.0)
    step_row = lax.broadcasted_iota(jnp.int32, (steps, channels), 0)

    def tables(a, carry):
        bc, bs = base_cos[pl.ds(a, 1), :], base_sin[pl.ds(a, 1), :]
        uc, us = step_cos[...], step_sin[...]
        at = pl.multiple_of(a * steps, steps)
        table[pl.ds(at, steps), :] = (uc * bc - us * bs).astype(BF16)
        sines = jnp.where(step_row + at == 0, middle, us * bc + uc * bs)
        table[pl.ds(half + at, steps), :] = sines.astype(BF16)
        return carry

    lax.fori_loop(0, bases, tables, 0)
    cov_copy.wait()
    tall = 256

    def folding(i, carry):
        at = pl.ds(pl.multiple_of(i * tall, tall), tall)
        fold[at, :] = dot(table[at, :], cov[...]).astype(BF16)
        return carry

    folds = channels // tall
    ahead_folds = folds - nz // 2
    lax.fori_loop(0, ahead_folds, folding, 0)

    def pass_on(q):
        for j in range(1, nx):
            f_copy(q, j).start()

    def folding_on(i, carry):
        q = 2 * (i - ahead_folds)
        p_copy(q).wait_recv()
        pass_on(q)

        @pl.when(q + 1 < last)
        def _():
            p_copy(q + 1).wait_recv()

        @pl.when(q + 1 == last)
        def _():
            own_p.wait()

        pass_on(q + 1)
        return folding(i, carry)

    lax.fori_loop(ahead_folds, folds, folding_on, 0)

    def swap(v, w):
        if w < LANES:
            return pltpu.roll(v, w, 1)
        return jnp.concatenate([v[:, w:], v[:, :w]], axis=1)

    def partial(h, rows, member, w):
        at = pl.multiple_of(h * part, part)
        c = dot(fold[pl.ds(at, part), :], rows[...])
        s = dot(fold[pl.ds(half + at, part), :], rows[...])
        first = lax.broadcasted_iota(jnp.int32, (part, 1), 0) + at == 0
        mine = member[...]

        def total(v):
            return dot(v, mine, NT)

        def exact(v):
            top = v.astype(BF16)
            return total(top) + total((v - top.astype(F32)).astype(BF16))

        if w < LANES:
            cr, sr = swap(c, w), swap(s, w)
            even, odd = c * c + cr * cr, s * s + sr * sr
            cross = 2.0 * (c * sr - cr * s)
            lane = lax.broadcasted_iota(jnp.int32, (1, 2 * w), 1)
            powers = jnp.where(first, jnp.where(lane < w, even, odd), even + odd + cross)
        else:
            rc, ic, rs, im = c[:, :w], c[:, w:], s[:, :w], s[:, w:]
            even, odd = rc * rc + ic * ic, rs * rs + im * im
            cross = 2.0 * (rc * im - ic * rs)
            powers = jnp.concatenate(
                [jnp.where(first, even, even + odd + cross), jnp.where(first, odd, even + odd - cross)],
                axis=1,
            )
        return exact(c), exact(s), total(powers.astype(BF16)), first

    own_a.wait()
    others(lambda q, i: a_copy(q, i).wait_recv())

    def part_a(h, carry):
        at = pl.ds(pl.multiple_of(h * part, part), part)
        for n, v in enumerate(partial(h, rows_a, member_a, cap)[:3]):
            sums[n, at, :] = v
        return carry

    lax.fori_loop(0, spans, part_a, 0)

    def forwarded(q, carry):
        for j in range(1, nx):
            f_copy(q, j).wait_recv()
        return carry

    lax.fori_loop(0, nz, forwarded, 0)

    def part_p(h, carry):
        at = pl.ds(pl.multiple_of(h * part, part), part)
        for n, v in enumerate(partial(h, rows_p, member_p, LANES)[:3]):
            sums[n, at, :] += v
        return carry

    lax.fori_loop(0, spans, part_p, 0)
    own_b.wait()
    others(lambda q, i: b_copy(q, i).wait_recv())

    def share_copy(source, h, to, dl):
        return pltpu.make_async_remote_copy(
            src_ref=source.at[h],
            dst_ref=landed.at[lst],
            send_sem=y_send.at[to],
            recv_sem=y_recv.at[dl],
            device_id=(to, chan),
            device_id_type=MESH,
        )

    def share(source, h, to):
        @pl.when(to != lst)
        def _():
            share_copy(source, h, to, lax.rem(to - lst + nl, nl)).start()

        @pl.when(to == lst)
        def _():
            landed[lst] = source[h]

    tall_share = part // 2
    below = lax.broadcasted_iota(jnp.int32, (part, LANES), 1) < held
    for h in range(spans):
        share_plus[h, pl.ds(tall_share, TAIL), :] = jnp.zeros((TAIL, LANES), BF16)

    def finish(h, carry):
        at = pl.ds(pl.multiple_of(h * part, part), part)
        c, s, p, first = partial(h, rows_b, member_b, held)
        c, s, p = c + sums[0, at, :], s + sums[1, at, :], p + sums[2, at, :]
        turned = jnp.where(below, 1.0, -1.0) * pltpu.roll(s, held, 1)
        up = jnp.where(first, c, c + turned)
        down = jnp.where(first, s, c - turned)
        up, down = up * up, down * down
        whole = jnp.where(below, up + pltpu.roll(up, held, 1), down + pltpu.roll(down, held, 1))
        crossed = (whole - p) * scale_ref[:1, :]
        top, bottom = crossed[:tall_share], crossed[tall_share:]
        under = below[:tall_share]
        share_plus[h, pl.ds(0, tall_share), :] = jnp.where(
            under, top, pltpu.roll(bottom, held, 1)
        ).astype(BF16)
        minus = jnp.where(under, pltpu.roll(top, held, 1), bottom).astype(BF16)
        share_minus[h, pl.ds(0, tall_share), :] = minus

        @pl.when(h == 0)
        def _():
            share_minus[spans - 1, pl.ds(tall_share, TAIL), :] = minus[:TAIL]

        @pl.when(h > 0)
        def _():
            share_minus[h - 1, pl.ds(tall_share, TAIL), :] = minus[:TAIL]
            share(share_plus, h - 1, h - 1)

        @pl.when(h > 1)
        def _():
            share(share_minus, h - 2, nl + 1 - h)

        return carry

    lax.fori_loop(0, spans, finish, 0)
    share(share_plus, spans - 1, spans - 1)
    share(share_minus, spans - 2, nl + 1 - spans)
    share(share_minus, spans - 1, nl - spans)

    row = lax.broadcasted_iota(jnp.int32, (tall_share + TAIL, part), 0)
    col = lax.broadcasted_iota(jnp.int32, (tall_share + TAIL, part), 1)
    want = jnp.where(lst < spans, col, part - col)
    lower = one_if((row == want) & (row < tall_share) | (row == want - tall_share) & (want == part))
    upper = one_if((row + tall_share == want) & (row < tall_share))
    turn = jnp.concatenate([lower, upper], axis=1)

    def order(t):
        both = dot(landed[t], turn, TN)
        pieces[t] = both[:held, :part] + both[held:, part:]

    order(lst)
    for dl in range(1, nl):
        bin_copy(dl).wait()
        share_copy(share_plus, 0, lax.rem(lst + dl, nl), dl).wait_recv()
        order(lax.rem(lst + nl - dl, nl))
    codes = [bin_land[t].astype(F32)[:1, :1] for t in range(nl)]
    for b in range(NBIN):
        total = jnp.zeros((held, part), F32)
        count = jnp.zeros((1, 1), F32)
        for t in range(nl):
            inside = codes[t] == b
            total += jnp.where(inside, pieces[t], 0.0)
            count += jnp.where(inside, 1.0, 0.0)
        out_ref[b] = total * (1.0 / jnp.maximum(count, 1.0))

    others(lambda q, i: a_copy(q, i).wait_send())
    others(lambda q, i: b_copy(q, i).wait_send())

    def sent(q, carry):
        for j in range(1, nx):
            f_copy(q, j).wait_send()

        @pl.when(q < last)
        def _():
            p_copy(q).wait_send()

        return carry

    lax.fori_loop(0, nz, sent, 0)
    for dl in range(1, nl):
        share_copy(share_plus, 0, lax.rem(lst + dl, nl), dl).wait_send()


def cross_power(cap, collective_id, sizes, lst_bin, owner, size, vis, cov):
    nx, nz, nl, held, channels, width = sizes
    half = channels // 2
    part = channels // nl
    total = nx * nz
    vmem = pltpu.VMEM
    dma = pltpu.SemaphoreType.DMA
    share = (channels // (2 * part), part // 2 + TAIL, LANES)
    return pl.pallas_call(
        functools.partial(kernel, cap, sizes),
        out_shape=jax.ShapeDtypeStruct((NBIN, held, part), F32),
        in_specs=[
            pl.BlockSpec(memory_space=pltpu.SMEM),
            pl.BlockSpec(memory_space=vmem),
            pl.BlockSpec(memory_space=vmem),
            pl.BlockSpec(memory_space=vmem),
            pl.BlockSpec(memory_space=pl.ANY),
        ],
        out_specs=pl.BlockSpec(memory_space=vmem),
        scratch_shapes=[
            vmem((channels, channels), BF16),
            vmem((nx * held, owner.shape[1]), BF16),
            vmem((SLOT * held, cap + 2 * LANES), BF16),
            vmem((2 * SLOT * width, nx * held), F32),
            vmem((nx, 2 * width, SLOT * held), BF16),
            vmem((total, width, 2 * cap), BF16),
            vmem((total, width, LANES), BF16),
            vmem((nz, width, 2 * LANES), BF16),
            vmem((channels, 2 * cap), BF16),
            vmem((channels, LANES), BF16),
            vmem((channels, 2 * LANES), BF16),
            vmem((channels, channels), BF16),
            vmem((channels, channels), BF16),
            vmem((64, channels), F32),
            vmem((64, channels), F32),
            vmem((16, channels), F32),
            vmem((16, channels), F32),
            vmem((2 * held, 2 * cap), BF16),
            vmem((2 * held, LANES), BF16),
            vmem((2 * held, 2 * LANES), BF16),
            vmem((8, LANES), F32),
            vmem((3, half, LANES), F32),
            vmem(share, BF16),
            vmem(share, BF16),
            vmem((nl,) + share[1:], BF16),
            vmem((nl, held, part), F32),
            vmem((16, LANES), BF16),
            vmem((nl, 16, LANES), BF16),
            dma(()),
            dma((3,)),
            dma((total,)),
            dma((total,)),
            dma((total,)),
            dma((total,)),
            dma((nz,)),
            dma((nz,)),
            dma((nz * (nx - 1),)),
            dma((nz * (nx - 1),)),
            dma((nl,)),
            dma((nl,)),
            dma((nl,)),
            dma((nl,)),
        ],
        compiler_params=pltpu.CompilerParams(
            collective_id=collective_id, has_side_effects=True, vmem_limit_bytes=60 * 2**20
        ),
    )(lst_bin, owner, size, vis, cov)


def solution(mesh):
    nl, total = mesh.shape["lst"], mesh.shape["chan"]
    nx = total // 8
    nz = total // nx

    def shards(visibility, inverse_cov, group_size, group_owner, lst_bin):
        groups, width = visibility.shape[2], visibility.shape[4]
        channels = inverse_cov.shape[0]
        held = groups // total
        sizes = (nx, nz, nl, held, channels, width)
        vis = jnp.transpose(visibility, (0, 1, 3, 4, 2)).reshape(2 * SLOT * width, groups)
        owner = group_owner.reshape(1, groups)
        size = group_size.reshape(1, groups)
        full = SLOT * held
        tight = full // 2
        fits = pl.pallas_call(
            functools.partial(fits_kernel, tight + held, LANES, sizes),
            out_shape=jax.ShapeDtypeStruct((1,), jnp.int32),
            out_specs=pl.BlockSpec(memory_space=pltpu.SMEM),
        )(owner, size)
        return lax.cond(
            fits[0] > 0,
            functools.partial(cross_power, tight, 0, sizes),
            functools.partial(cross_power, full, 1, sizes),
            lst_bin, owner, size, vis, inverse_cov,
        )

    placed = (P(None, "lst", None, None, "chan"), P(), P(), P(), P("lst"))
    return jax.shard_map(
        shards, mesh=mesh, in_specs=placed, out_specs=P(None, "chan", "lst"), check_vma=False
    )
```

time: 84.3 us -> 81.1 us (0.962); the launches traced: 84.1 us -> 79.7 us
  other arithmetic: 2.18 us -> 0 us
  Pallas kernels: 80 us -> 78.1 us
    pallas_call x1, Pallas kernels: 80 us -> 76.7 us  [cross_power(): pl.pallas_call(functools.partial(kernel, cap, sizes), out_shape=jax.Shape...]
    pallas_call x0 -> x1, Pallas kernels: none -> 1.42 us  [shards(): pl.pallas_call(functools.partial(fits_kernel, tight + held, LANES, sizes)...]
where the time goes in v2:
time: 81.1 us; the launch traced here: 79.7 us
  Pallas kernels  78.1 us (96%)
    pallas_call x1, Pallas kernels, cross_power(): pl.pallas_call(functools.partial(kernel, cap, sizes), out_shape=jax.Shape...  76.7 us

profile of v2, /device:TPU:1, one launch (start us, length us, event | category | flops | bytes accessed | tf_op | source)
XLA Modules:
  0.0 79.7 jit_solution(4295903493700353588)
XLA Ops:
  0.0 1.4 %shard_map.61 = s32[1]{0:T(128)} custom-call(s32[1,2048]{1,0:T(1,128)} %bitcast.12, s32[1,2048]{1,0:T(1,128)} %bitcast.15), custom_call_target="tpu_custom_call" | custom-call | tf_op jit(solution)/shard_map/pallas_call | solution.py:677
  2.1 76.9 %conditional.1 = (f32[8,64,192]{2,1,0:T(8,128)S(1)}) conditional(s32[]{:T(128)} %bitcast.4, (s32[1]{0:T(128)}, s32[1,2048]{1,0:T(1,128)}, s32[1,2048]{1,0:T(1,128)}, bf16[2,1,8,48,2048]{4,3,2,0,1:T(8,128)(2,1)}, bf16[1536,1536]{1,0:T(8,128)(2,1)}) %tuple.20, (s32[1]{0:T(128)}, s32[1,2048]{1,0:T(1,128)}, s32[1,2048]{1,0:T(1,128)}, ...), branch_computations={%region_0.0_spmd, %region_1.0_spmd} | conditional | bytes 8 | solution.py:682
  2.3 76.7 %branch_1_fun.1 = f32[8,64,192]{2,1,0:T(8,128)S(1)} custom-call(s32[1]{0:T(128)} %get-tuple-element.46.bin_ref, s32[1,2048]{1,0:T(1,128)} %get-tuple-element.34.owner_ref, s32[1,2048]{1,0:T(1,128)} %get-tuple-element.35.size_ref, bf16[768,2048]{1,0:T(8,128)(2,1)} %bitcast.11, bf16[1536,1536]{1,0:T(8,128)(2,1)} %get-tuple-element.48.cov_hbm), custom_call_target="tpu_custom_call" | custom-call | tf_op jit(solution)/shard_map/cond/branch_1_fun/pallas_call | solution.py:601
  78.9 0.8 copy.16

commit v3 on v2

--- a/solution.py
+++ b/solution.py
@@ -44,9 +44,11 @@
     bin_ref,
     owner_ref,
     size_ref,
-    vis_ref,
+    vis_hbm,
     cov_hbm,
     out_ref,
+    vis,
+    vis_sem,
     cov,
     pick,
     chosen,
@@ -68,7 +70,9 @@
     member_b,
     member_p,
     scale_ref,
+    held_ref,
     sums,
+    acc_b,
     share_plus,
     share_minus,
     landed,
@@ -115,8 +119,8 @@
         return pltpu.make_async_remote_copy(
             src_ref=send_a.at[n],
             dst_ref=rows_of(rows_a, chan),
-            send_sem=a_send.at[n],
-            recv_sem=a_recv.at[n],
+            send_sem=a_send,
+            recv_sem=a_recv,
             device_id=(lst, place(q, i)),
             device_id_type=MESH,
         )
@@ -126,8 +130,8 @@
         return pltpu.make_async_remote_copy(
             src_ref=send_b.at[n],
             dst_ref=rows_of(rows_b, chan),
-            send_sem=b_send.at[n],
-            recv_sem=b_recv.at[n],
+            send_sem=b_send,
+            recv_sem=b_recv.at[i],
             device_id=(lst, place(q, i)),
             device_id_type=MESH,
         )
@@ -136,7 +140,7 @@
         return pltpu.make_async_remote_copy(
             src_ref=send_p.at[q],
             dst_ref=rows_of(rows_p, chan),
-            send_sem=p_send.at[q],
+            send_sem=p_send,
             recv_sem=p_recv.at[q],
             device_id=(lst, place(q, 0)),
             device_id_type=MESH,
@@ -144,12 +148,11 @@
 
     def f_copy(q, j):
         source = x * nz + lax.rem(z + nz - ahead(q), nz)
-        n = (nx - 1) * q + j - 1
         return pltpu.make_async_remote_copy(
             src_ref=rows_of(rows_p, source),
             dst_ref=rows_of(rows_p, source),
-            send_sem=f_send.at[n],
-            recv_sem=f_recv.at[n],
+            send_sem=f_send,
+            recv_sem=f_recv,
             device_id=(lst, lax.rem(x + j, nx) * nz + z),
             device_id_type=MESH,
         )
@@ -159,6 +162,8 @@
     own_p = pltpu.make_async_copy(send_p.at[last], rows_of(rows_p, chan), own_sem.at[2])
     cov_copy = pltpu.make_async_copy(cov_hbm, cov, cov_sem)
 
+    vis_copy = pltpu.make_async_copy(vis_hbm, vis, vis_sem)
+    vis_copy.start()
     barrier = pltpu.get_barrier_semaphore()
     for other in range(1, nx * nz):
         peer = lax.rem(x + other // nz, nx) * nz + lax.rem(z + other % nz, nz)
@@ -167,7 +172,6 @@
         pl.semaphore_signal(
             barrier, inc=1, device_id=(lax.rem(lst + dl, nl), chan), device_id_type=MESH
         )
-    cov_copy.start()
 
     low = lax.broadcasted_iota(jnp.int32, (width, LANES), 1) < held
     lane = lax.broadcasted_iota(jnp.int32, (1, wide), 1)
@@ -215,10 +219,22 @@
                 live_sum += jnp.where(hit, sizes_here, none)
             lives.append(jnp.sum(live_sum.astype(F32), axis=1, keepdims=True))
         live = jnp.concatenate(lives, axis=0)
+        if not first:
+            for i in range(nx - 1):
+
+                @pl.when(q > 1)
+                def _():
+                    a_copy(q - 1, i).start()
+
+            a_copy(q - 1, nx - 1).start()
+            p_copy(q - 1).start()
         live_wide = jnp.broadcast_to(live, (nx * held, LANES)).astype(BF16)
         start = dot(before, live_wide)[:, :1].astype(jnp.int32)
         live = live.astype(jnp.int32)
-        gathered[...] = dot(vis_ref[...], pick[...], NT)
+        if first:
+            vis_copy.wait()
+            cov_copy.start()
+        gathered[...] = dot(vis[...], pick[...], NT)
         for i in range(nx):
             for c in range(2):
                 for pair in range(SLOT // 2):
@@ -250,10 +266,14 @@
             slot = rank - start_i
             slot = jnp.where((slot < live_i) & (rank >= 0), slot, -1).astype(F32).astype(BF16)
             for s in range(SLOT):
-                chosen[pl.ds(s * held, held), :] = jnp.where(
+                chosen[i, pl.ds(s * held, held), :] = jnp.where(
                     slot == float(s), jnp.ones_like(slot), jnp.zeros_like(slot)
                 )
-            block = dot(paired[i], chosen[...])
+            block = dot(paired[i], chosen[i])
+            if i == 0:
+                held_ref[0] = jnp.broadcast_to(live_i, (held, LANES))
+                held_ref[1] = jnp.broadcast_to(start_i, (held, LANES))
+                held_ref[2] = jnp.broadcast_to(pooled, (held, LANES))
             n = nx * q + i
             send_a[n, :, pl.ds(0, cap)] = block[:width, :cap].astype(BF16)
             send_a[n, :, pl.ds(cap, cap)] = block[width:, :cap].astype(BF16)
@@ -261,36 +281,13 @@
             send_b[n] = jnp.where(low, re, pltpu.roll(im, held, 1)).astype(BF16)
             extra = block[:, cap + LANES :]
             pool = extra if pool is None else pool + extra
-            if first:
-                if i == 1:
-                    pl.semaphore_wait(barrier, nx * nz - 1 + nl - 1)
-                if i > 0:
-                    a_copy(q, i - 1).start()
-            elif i == 0:
-                a_copy(q - 1, nx - 1).start()
-                p_copy(q - 1).start()
-
-                @pl.when(q == last)
-                def _():
-                    members(start_i, live_i, pooled)
-
-            elif i == 1:
-
-                @pl.when(q < last)
-                def _():
-                    a_copy(q, 0).start()
-
-                @pl.when(q == last)
-                def _():
-                    own_a.start()
-                    own_b.start()
-
-            else:
-                a_copy(q, i - 1).start()
         send_p[q, :, pl.ds(0, LANES)] = pool[:width].astype(BF16)
         send_p[q, :, pl.ds(LANES, LANES)] = pool[width:].astype(BF16)
 
     column(0, True)
+    pl.semaphore_wait(barrier, nx * nz - 1 + nl - 1)
+    for i in range(nx - 1):
+        a_copy(0, i).start()
 
     def later(q, carry):
         column(q, False)
@@ -298,32 +295,31 @@
 
     lax.fori_loop(1, nz, later, 0)
     bin_send[...] = jnp.full(bin_send.shape, bin_ref[0], jnp.int32).astype(F32).astype(BF16)
-    a_copy(last, nx - 1).start()
+    for i in range(1, nx):
+        a_copy(last, i).start()
+    own_a.start()
+    own_b.start()
     own_p.start()
 
-    def others(each):
-        def some(q, carry):
-            for i in range(nx):
-                if i > 0:
-                    each(q, i)
-                else:
-
-                    @pl.when(q < last)
-                    def _():
-                        each(q, 0)
-
+    def await_all(like, semaphore):
+        pltpu.make_async_copy(like, like, semaphore).wait()
+
+    blocks = nx * nz - 1
+    for i in (1, 2, 3, 0):
+
+        def start_b(q, carry):
+            b_copy(q, i).start()
             return carry
 
-        lax.fori_loop(0, nz, some, 0)
-
-    others(lambda q, i: b_copy(q, i).start())
+        lax.fori_loop(0, nz - (i == 0), start_b, 0)
+    members(held_ref[1][:, :1], held_ref[0][:, :1], held_ref[2][:1, :1])
 
     def bin_copy(dl):
         return pltpu.make_async_remote_copy(
             src_ref=bin_send,
             dst_ref=bin_land.at[lst],
-            send_sem=n_send.at[dl],
-            recv_sem=n_recv.at[dl],
+            send_sem=n_send,
+            recv_sem=n_recv,
             device_id=(lax.rem(lst + dl, nl), chan),
             device_id_type=MESH,
         )
@@ -427,9 +423,13 @@
         return jnp.concatenate([v[:, w:], v[:, :w]], axis=1)
 
     def partial(h, rows, member, w):
-        at = pl.multiple_of(h * part, part)
-        c = dot(fold[pl.ds(at, part), :], rows[...])
-        s = dot(fold[pl.ds(half + at, part), :], rows[...])
+        at = h * part if isinstance(h, int) else pl.multiple_of(h * part, part)
+        if rows is None:
+            c = acc_b[pl.ds(at, part), :]
+            s = acc_b[pl.ds(half + at, part), :]
+        else:
+            c = dot(fold[pl.ds(at, part), :], rows[...])
+            s = dot(fold[pl.ds(half + at, part), :], rows[...])
         first = lax.broadcasted_iota(jnp.int32, (part, 1), 0) + at == 0
         mine = member[...]
 
@@ -457,7 +457,7 @@
         return exact(c), exact(s), total(powers.astype(BF16)), first
 
     own_a.wait()
-    others(lambda q, i: a_copy(q, i).wait_recv())
+    await_all(send_a.at[pl.ds(0, blocks)], a_recv)
 
     def part_a(h, carry):
         at = pl.ds(pl.multiple_of(h * part, part), part)
@@ -467,12 +467,8 @@
 
     lax.fori_loop(0, spans, part_a, 0)
 
-    def forwarded(q, carry):
-        for j in range(1, nx):
-            f_copy(q, j).wait_recv()
-        return carry
-
-    lax.fori_loop(0, nz, forwarded, 0)
+    relayed = rows_p.at[pl.ds(0, nz * (nx - 1) * width), :]
+    await_all(relayed, f_recv)
 
     def part_p(h, carry):
         at = pl.ds(pl.multiple_of(h * part, part), part)
@@ -481,15 +477,29 @@
         return carry
 
     lax.fori_loop(0, spans, part_p, 0)
-    own_b.wait()
-    others(lambda q, i: b_copy(q, i).wait_recv())
-
-    def share_copy(source, h, to, dl):
+    await_all(send_a.at[pl.ds(0, blocks)], a_send)
+    await_all(send_p.at[pl.ds(0, last)], p_send)
+    await_all(relayed, f_send)
+    await_all(bin_land.at[pl.ds(0, nl - 1)], n_send)
+    await_all(bin_land.at[pl.ds(0, nl - 1)], n_recv)
+    deep = nz * width
+    for i in (1, 2, 3, 0):
+        await_all(send_b.at[pl.ds(0, nz - (i == 0))], b_recv.at[i])
+        if i == 0:
+            own_b.wait()
+        ch = pl.ds(pl.multiple_of(lax.rem(x + nx - i, nx) * deep, deep), deep)
+        term = dot(fold[:, ch], rows_b[ch, :])
+        if i == 1:
+            acc_b[...] = term
+        else:
+            acc_b[...] += term
+
+    def share_copy(source, h, to):
         return pltpu.make_async_remote_copy(
             src_ref=source.at[h],
             dst_ref=landed.at[lst],
-            send_sem=y_send.at[to],
-            recv_sem=y_recv.at[dl],
+            send_sem=y_send,
+            recv_sem=y_recv,
             device_id=(to, chan),
             device_id_type=MESH,
         )
@@ -497,7 +507,7 @@
     def share(source, h, to):
         @pl.when(to != lst)
         def _():
-            share_copy(source, h, to, lax.rem(to - lst + nl, nl)).start()
+            share_copy(source, h, to).start()
 
         @pl.when(to == lst)
         def _():
@@ -508,9 +518,9 @@
     for h in range(spans):
         share_plus[h, pl.ds(tall_share, TAIL), :] = jnp.zeros((TAIL, LANES), BF16)
 
-    def finish(h, carry):
-        at = pl.ds(pl.multiple_of(h * part, part), part)
-        c, s, p, first = partial(h, rows_b, member_b, held)
+    def finish(h):
+        at = pl.ds(h * part, part)
+        c, s, p, first = partial(h, None, member_b, held)
         c, s, p = c + sums[0, at, :], s + sums[1, at, :], p + sums[2, at, :]
         turned = jnp.where(below, 1.0, -1.0) * pltpu.roll(s, held, 1)
         up = jnp.where(first, c, c + turned)
@@ -526,25 +536,18 @@
         minus = jnp.where(under, pltpu.roll(top, held, 1), bottom).astype(BF16)
         share_minus[h, pl.ds(0, tall_share), :] = minus
 
-        @pl.when(h == 0)
-        def _():
-            share_minus[spans - 1, pl.ds(tall_share, TAIL), :] = minus[:TAIL]
-
-        @pl.when(h > 0)
-        def _():
-            share_minus[h - 1, pl.ds(tall_share, TAIL), :] = minus[:TAIL]
-            share(share_plus, h - 1, h - 1)
-
-        @pl.when(h > 1)
-        def _():
-            share(share_minus, h - 2, nl + 1 - h)
-
-        return carry
-
-    lax.fori_loop(0, spans, finish, 0)
-    share(share_plus, spans - 1, spans - 1)
-    share(share_minus, spans - 2, nl + 1 - spans)
-    share(share_minus, spans - 1, nl - spans)
+        share_minus[(h - 1) % spans, pl.ds(tall_share, TAIL), :] = minus[:TAIL]
+
+    for h in range(spans):
+        if h == 2:
+            share(share_plus, 0, 0)
+            share(share_plus, 1, 1)
+            share(share_minus, 0, nl - 1)
+        finish(h)
+    for h in range(2, spans):
+        share(share_plus, h, h)
+    for h in range(1, spans):
+        share(share_minus, h, nl - 1 - h)
 
     row = lax.broadcasted_iota(jnp.int32, (tall_share + TAIL, part), 0)
     col = lax.broadcasted_iota(jnp.int32, (tall_share + TAIL, part), 1)
@@ -557,11 +560,11 @@
         both = dot(landed[t], turn, TN)
         pieces[t] = both[:held, :part] + both[held:, part:]
 
+    await_all(send_b.at[pl.ds(0, blocks)], b_send)
     order(lst)
+    await_all(landed.at[pl.ds(0, nl - 1)], y_recv)
     for dl in range(1, nl):
-        bin_copy(dl).wait()
-        share_copy(share_plus, 0, lax.rem(lst + dl, nl), dl).wait_recv()
-        order(lax.rem(lst + nl - dl, nl))
+        order(lax.rem(lst + dl, nl))
     codes = [bin_land[t].astype(F32)[:1, :1] for t in range(nl)]
     for b in range(NBIN):
         total = jnp.zeros((held, part), F32)
@@ -572,22 +575,7 @@
             count += jnp.where(inside, 1.0, 0.0)
         out_ref[b] = total * (1.0 / jnp.maximum(count, 1.0))
 
-    others(lambda q, i: a_copy(q, i).wait_send())
-    others(lambda q, i: b_copy(q, i).wait_send())
-
-    def sent(q, carry):
-        for j in range(1, nx):
-            f_copy(q, j).wait_send()
-
-        @pl.when(q < last)
-        def _():
-            p_copy(q).wait_send()
-
-        return carry
-
-    lax.fori_loop(0, nz, sent, 0)
-    for dl in range(1, nl):
-        share_copy(share_plus, 0, lax.rem(lst + dl, nl), dl).wait_send()
+    await_all(landed.at[pl.ds(0, nl - 1)], y_send)
 
 
 def cross_power(cap, collective_id, sizes, lst_bin, owner, size, vis, cov):
@@ -605,14 +593,16 @@
             pl.BlockSpec(memory_space=pltpu.SMEM),
             pl.BlockSpec(memory_space=vmem),
             pl.BlockSpec(memory_space=vmem),
-            pl.BlockSpec(memory_space=vmem),
+            pl.BlockSpec(memory_space=pl.ANY),
             pl.BlockSpec(memory_space=pl.ANY),
         ],
         out_specs=pl.BlockSpec(memory_space=vmem),
         scratch_shapes=[
+            vmem(vis.shape, BF16),
+            dma(()),
             vmem((channels, channels), BF16),
             vmem((nx * held, owner.shape[1]), BF16),
-            vmem((SLOT * held, cap + 2 * LANES), BF16),
+            vmem((nx, SLOT * held, cap + 2 * LANES), BF16),
             vmem((2 * SLOT * width, nx * held), F32),
             vmem((nx, 2 * width, SLOT * held), BF16),
             vmem((total, width, 2 * cap), BF16),
@@ -631,7 +621,9 @@
             vmem((2 * held, LANES), BF16),
             vmem((2 * held, 2 * LANES), BF16),
             vmem((8, LANES), F32),
+            vmem((3, held, LANES), jnp.int32),
             vmem((3, half, LANES), F32),
+            vmem((channels, LANES), F32),
             vmem(share, BF16),
             vmem(share, BF16),
             vmem((nl,) + share[1:], BF16),
@@ -640,18 +632,18 @@
             vmem((nl, 16, LANES), BF16),
             dma(()),
             dma((3,)),
-            dma((total,)),
-            dma((total,)),
-            dma((total,)),
-            dma((total,)),
+            dma(()),
+            dma(()),
+            dma(()),
+            dma((nx,)),
+            dma(()),
             dma((nz,)),
-            dma((nz,)),
-            dma((nz * (nx - 1),)),
-            dma((nz * (nx - 1),)),
-            dma((nl,)),
-            dma((nl,)),
-            dma((nl,)),
-            dma((nl,)),
+            dma(()),
+            dma(()),
+            dma(()),
+            dma(()),
+            dma(()),
+            dma(()),
         ],
         compiler_params=pltpu.CompilerParams(
             collective_id=collective_id, has_side_effects=True, vmem_limit_bytes=60 * 2**20

time: 81.1 us -> 77.3 us (0.953); the launches traced: 79.7 us -> 77 us
  Pallas kernels: 78.1 us -> 75.3 us
    pallas_call x1, Pallas kernels: 76.7 us -> 73.9 us  [cross_power(): pl.pallas_call(functools.partial(kernel, cap, sizes), out_shape=jax.Shape...]
where the time goes in v3:
time: 77.3 us; the launch traced here: 77 us
  Pallas kernels  75.3 us (97%)
  local copies, waits for them, and re-layouts  0.8 us (1%)
    pallas_call x1, Pallas kernels, cross_power(): pl.pallas_call(functools.partial(kernel, cap, sizes), out_shape=jax.Shape...  73.9 us

profile of v3, /device:TPU:1, one launch (start us, length us, event | category | flops | bytes accessed | tf_op | source)
XLA Modules:
  0.0 77.0 jit_solution(14846365758357079979)
XLA Ops:
  0.0 1.4 %shard_map.61 = s32[1]{0:T(128)} custom-call(s32[1,2048]{1,0:T(1,128)} %bitcast.12, s32[1,2048]{1,0:T(1,128)} %bitcast.15), custom_call_target="tpu_custom_call" | custom-call | tf_op jit(solution)/shard_map/pallas_call | solution.py:669
  2.1 74.1 %conditional.1 = (f32[8,64,192]{2,1,0:T(8,128)S(1)}) conditional(s32[]{:T(128)} %bitcast.4, (s32[1]{0:T(128)}, s32[1,2048]{1,0:T(1,128)}, s32[1,2048]{1,0:T(1,128)}, bf16[2,1,8,48,2048]{4,3,2,0,1:T(8,128)(2,1)}, bf16[1536,1536]{1,0:T(8,128)(2,1)}) %tuple.20, (s32[1]{0:T(128)}, s32[1,2048]{1,0:T(1,128)}, s32[1,2048]{1,0:T(1,128)}, ...), branch_computations={%region_0.0_spmd, %region_1.0_spmd} | conditional | bytes 8 | solution.py:674
  2.3 73.9 %branch_1_fun.1 = f32[8,64,192]{2,1,0:T(8,128)S(1)} custom-call(s32[1]{0:T(128)} %get-tuple-element.46.bin_ref, s32[1,2048]{1,0:T(1,128)} %get-tuple-element.34.owner_ref, s32[1,2048]{1,0:T(1,128)} %get-tuple-element.35.size_ref, bf16[768,2048]{1,0:T(8,128)(2,1)} %bitcast.11, bf16[1536,1536]{1,0:T(8,128)(2,1)} %get-tuple-element.48.cov_hbm), custom_call_target="tpu_custom_call" | custom-call | tf_op jit(solution)/shard_map/cond/branch_1_fun/pallas_call | solution.py:589
  76.2 0.8 %copy.16 = f32[8,64,192]{2,1,0:T(8,128)} copy(f32[8,64,192]{2,1,0:T(8,128)S(1)} %get-tuple-element.38) | data formatting | bytes 786432

commit v4 on v3

--- a/solution.py
+++ b/solution.py
@@ -54,9 +54,11 @@
     chosen,
     gathered,
     paired,
+    send_h,
     send_a,
     send_b,
     send_p,
+    rows_h,
     rows_a,
     rows_b,
     rows_p,
@@ -66,6 +68,7 @@
     step_sin,
     base_cos,
     base_sin,
+    member_h,
     member_a,
     member_b,
     member_p,
@@ -81,6 +84,8 @@
     bin_land,
     cov_sem,
     own_sem,
+    h_send,
+    h_recv,
     a_send,
     a_recv,
     b_send,
@@ -100,6 +105,7 @@
     spans = half // part
     base = cap + held
     wide = cap + 2 * LANES
+    rest = cap - LANES
     lst = lax.axis_index("lst")
     chan = lax.axis_index("chan")
     x, z = chan // nz, chan % nz
@@ -113,6 +119,17 @@
 
     def rows_of(ref, source):
         return ref.at[pl.ds(pl.multiple_of(source * width, 16), width), :]
+
+    def h_copy(q, i):
+        n = nx * q + i
+        return pltpu.make_async_remote_copy(
+            src_ref=send_h.at[n],
+            dst_ref=rows_of(rows_h, chan),
+            send_sem=h_send,
+            recv_sem=h_recv,
+            device_id=(lst, place(q, i)),
+            device_id_type=MESH,
+        )
 
     def a_copy(q, i):
         n = nx * q + i
@@ -157,6 +174,7 @@
             device_id_type=MESH,
         )
 
+    own_h = pltpu.make_async_copy(send_h.at[nx * last], rows_of(rows_h, chan), own_sem.at[3])
     own_a = pltpu.make_async_copy(send_a.at[nx * last], rows_of(rows_a, chan), own_sem.at[0])
     own_b = pltpu.make_async_copy(send_b.at[nx * last], rows_of(rows_b, chan), own_sem.at[1])
     own_p = pltpu.make_async_copy(send_p.at[last], rows_of(rows_p, chan), own_sem.at[2])
@@ -182,11 +200,15 @@
     one, none = jnp.ones((held, LANES), BF16), jnp.zeros((held, LANES), BF16)
 
     def members(start, live, pooled):
-        at = lax.broadcasted_iota(jnp.int32, (held, cap), 1)
-        mine = one_if((at >= start) & (at < start + live))
-        empty = jnp.zeros((held, cap), BF16)
-        member_a[pl.ds(0, held), :] = jnp.concatenate([mine, empty], axis=1)
-        member_a[pl.ds(held, held), :] = jnp.concatenate([empty, mine], axis=1)
+        def spread_out(member, w, offset):
+            at = lax.broadcasted_iota(jnp.int32, (held, w), 1) + offset
+            mine = one_if((at >= start) & (at < start + live))
+            empty = jnp.zeros((held, w), BF16)
+            member[pl.ds(0, held), :] = jnp.concatenate([mine, empty], axis=1)
+            member[pl.ds(held, held), :] = jnp.concatenate([empty, mine], axis=1)
+
+        spread_out(member_h, LANES, 0)
+        spread_out(member_a, rest, LANES)
         at = lax.broadcasted_iota(jnp.int32, (held, LANES), 1)
         below = at < held
         near = lax.rem(at, held) + cap
@@ -224,10 +246,16 @@
 
                 @pl.when(q > 1)
                 def _():
+                    h_copy(q - 1, i).start()
+
+            h_copy(q - 1, nx - 1).start()
+            p_copy(q - 1).start()
+
+            @pl.when(q <= nz // 2)
+            def _():
+                for i in range(nx):
                     a_copy(q - 1, i).start()
 
-            a_copy(q - 1, nx - 1).start()
-            p_copy(q - 1).start()
         live_wide = jnp.broadcast_to(live, (nx * held, LANES)).astype(BF16)
         start = dot(before, live_wide)[:, :1].astype(jnp.int32)
         live = live.astype(jnp.int32)
@@ -275,8 +303,10 @@
                 held_ref[1] = jnp.broadcast_to(start_i, (held, LANES))
                 held_ref[2] = jnp.broadcast_to(pooled, (held, LANES))
             n = nx * q + i
-            send_a[n, :, pl.ds(0, cap)] = block[:width, :cap].astype(BF16)
-            send_a[n, :, pl.ds(cap, cap)] = block[width:, :cap].astype(BF16)
+            send_h[n, :, pl.ds(0, LANES)] = block[:width, :LANES].astype(BF16)
+            send_h[n, :, pl.ds(LANES, LANES)] = block[width:, :LANES].astype(BF16)
+            send_a[n, :, pl.ds(0, rest)] = block[:width, LANES:cap].astype(BF16)
+            send_a[n, :, pl.ds(rest, rest)] = block[width:, LANES:cap].astype(BF16)
             re, im = block[:width, cap : cap + LANES], block[width:, cap : cap + LANES]
             send_b[n] = jnp.where(low, re, pltpu.roll(im, held, 1)).astype(BF16)
             extra = block[:, cap + LANES :]
@@ -287,7 +317,7 @@
     column(0, True)
     pl.semaphore_wait(barrier, nx * nz - 1 + nl - 1)
     for i in range(nx - 1):
-        a_copy(0, i).start()
+        h_copy(0, i).start()
 
     def later(q, carry):
         column(q, False)
@@ -296,7 +326,8 @@
     lax.fori_loop(1, nz, later, 0)
     bin_send[...] = jnp.full(bin_send.shape, bin_ref[0], jnp.int32).astype(F32).astype(BF16)
     for i in range(1, nx):
-        a_copy(last, i).start()
+        h_copy(last, i).start()
+    own_h.start()
     own_a.start()
     own_b.start()
     own_p.start()
@@ -305,6 +336,14 @@
         pltpu.make_async_copy(like, like, semaphore).wait()
 
     blocks = nx * nz - 1
+    def second_rows(q, carry):
+        for i in range(nx):
+            a_copy(q, i).start()
+        return carry
+
+    lax.fori_loop(nz // 2, last, second_rows, 0)
+    for i in range(1, nx):
+        a_copy(last, i).start()
     for i in (1, 2, 3, 0):
 
         def start_b(q, carry):
@@ -456,17 +495,26 @@
             )
         return exact(c), exact(s), total(powers.astype(BF16)), first
 
+    own_h.wait()
+    await_all(send_h.at[pl.ds(0, blocks)], h_recv)
+
+    def part_h(h, carry):
+        at = pl.ds(pl.multiple_of(h * part, part), part)
+        for n, v in enumerate(partial(h, rows_h, member_h, LANES)[:3]):
+            sums[n, at, :] = v
+        return carry
+
+    lax.fori_loop(0, spans, part_h, 0)
     own_a.wait()
     await_all(send_a.at[pl.ds(0, blocks)], a_recv)
 
     def part_a(h, carry):
         at = pl.ds(pl.multiple_of(h * part, part), part)
-        for n, v in enumerate(partial(h, rows_a, member_a, cap)[:3]):
-            sums[n, at, :] = v
+        for n, v in enumerate(partial(h, rows_a, member_a, rest)[:3]):
+            sums[n, at, :] += v
         return carry
 
     lax.fori_loop(0, spans, part_a, 0)
-
     relayed = rows_p.at[pl.ds(0, nz * (nx - 1) * width), :]
     await_all(relayed, f_recv)
 
@@ -477,6 +525,7 @@
         return carry
 
     lax.fori_loop(0, spans, part_p, 0)
+    await_all(send_h.at[pl.ds(0, blocks)], h_send)
     await_all(send_a.at[pl.ds(0, blocks)], a_send)
     await_all(send_p.at[pl.ds(0, last)], p_send)
     await_all(relayed, f_send)
@@ -605,10 +654,12 @@
             vmem((nx, SLOT * held, cap + 2 * LANES), BF16),
             vmem((2 * SLOT * width, nx * held), F32),
             vmem((nx, 2 * width, SLOT * held), BF16),
-            vmem((total, width, 2 * cap), BF16),
+            vmem((total, width, 2 * LANES), BF16),
+            vmem((total, width, 2 * (cap - LANES)), BF16),
             vmem((total, width, LANES), BF16),
             vmem((nz, width, 2 * LANES), BF16),
-            vmem((channels, 2 * cap), BF16),
+            vmem((channels, 2 * LANES), BF16),
+            vmem((channels, 2 * (cap - LANES)), BF16),
             vmem((channels, LANES), BF16),
             vmem((channels, 2 * LANES), BF16),
             vmem((channels, channels), BF16),
@@ -617,7 +668,8 @@
             vmem((64, channels), F32),
             vmem((16, channels), F32),
             vmem((16, channels), F32),
-            vmem((2 * held, 2 * cap), BF16),
+            vmem((2 * held, 2 * LANES), BF16),
+            vmem((2 * held, 2 * (cap - LANES)), BF16),
             vmem((2 * held, LANES), BF16),
             vmem((2 * held, 2 * LANES), BF16),
             vmem((8, LANES), F32),
@@ -631,7 +683,9 @@
             vmem((16, LANES), BF16),
             vmem((nl, 16, LANES), BF16),
             dma(()),
-            dma((3,)),
+            dma((4,)),
+            dma(()),
+            dma(()),
             dma(()),
             dma(()),
             dma(()),

time: 77.3 us -> 76.5 us (0.990)
  Pallas kernels: 75.3 us -> 74.5 us
    pallas_call x1, Pallas kernels: 73.9 us -> 73.1 us  [cross_power(): pl.pallas_call(functools.partial(kernel, cap, sizes), out_shape=jax.Shape...]
where the time goes in v4:
time: 76.5 us; the launch traced here: 76.2 us
  Pallas kernels  74.5 us (97%)
  local copies, waits for them, and re-layouts  0.8 us (1%)
    pallas_call x1, Pallas kernels, cross_power(): pl.pallas_call(functools.partial(kernel, cap, sizes), out_shape=jax.Shape...  73.1 us

profile of v4, /device:TPU:1, one launch (start us, length us, event | category | flops | bytes accessed | tf_op | source)
XLA Modules:
  0.0 76.2 jit_solution(8905751313844513120)
XLA Ops:
  0.0 1.4 %shard_map.61 = s32[1]{0:T(128)} custom-call(s32[1,2048]{1,0:T(1,128)} %bitcast.12, s32[1,2048]{1,0:T(1,128)} %bitcast.15), custom_call_target="tpu_custom_call" | custom-call | tf_op jit(solution)/shard_map/pallas_call | solution.py:723
  2.1 73.3 %conditional.1 = (f32[8,64,192]{2,1,0:T(8,128)S(1)}) conditional(s32[]{:T(128)} %bitcast.4, (s32[1]{0:T(128)}, s32[1,2048]{1,0:T(1,128)}, s32[1,2048]{1,0:T(1,128)}, bf16[2,1,8,48,2048]{4,3,2,0,1:T(8,128)(2,1)}, bf16[1536,1536]{1,0:T(8,128)(2,1)}) %tuple.20, (s32[1]{0:T(128)}, s32[1,2048]{1,0:T(1,128)}, s32[1,2048]{1,0:T(1,128)}, ...), branch_computations={%region_0.0_spmd, %region_1.0_spmd} | conditional | bytes 8 | solution.py:728
  2.3 73.1 %branch_1_fun.1 = f32[8,64,192]{2,1,0:T(8,128)S(1)} custom-call(s32[1]{0:T(128)} %get-tuple-element.46.bin_ref, s32[1,2048]{1,0:T(1,128)} %get-tuple-element.34.owner_ref, s32[1,2048]{1,0:T(1,128)} %get-tuple-element.35.size_ref, bf16[768,2048]{1,0:T(8,128)(2,1)} %bitcast.11, bf16[1536,1536]{1,0:T(8,128)(2,1)} %get-tuple-element.48.cov_hbm), custom_call_target="tpu_custom_call" | custom-call | tf_op jit(solution)/shard_map/cond/branch_1_fun/pallas_call | solution.py:638
  75.4 0.8 %copy.16 = f32[8,64,192]{2,1,0:T(8,128)} copy(f32[8,64,192]{2,1,0:T(8,128)S(1)} %get-tuple-element.38) | data formatting | bytes 786432

commit v5 on v4

--- a/solution.py
+++ b/solution.py
@@ -110,6 +110,7 @@
     chan = lax.axis_index("chan")
     x, z = chan // nz, chan % nz
     last = nz - 1
+    early = 1
 
     def ahead(q):
         return nz // 2 + (1 - 2 * (q % 2)) * ((q + 1) // 2)
@@ -251,7 +252,7 @@
             h_copy(q - 1, nx - 1).start()
             p_copy(q - 1).start()
 
-            @pl.when(q <= nz // 2)
+            @pl.when(q <= early)
             def _():
                 for i in range(nx):
                     a_copy(q - 1, i).start()
@@ -341,7 +342,7 @@
             a_copy(q, i).start()
         return carry
 
-    lax.fori_loop(nz // 2, last, second_rows, 0)
+    lax.fori_loop(early, last, second_rows, 0)
     for i in range(1, nx):
         a_copy(last, i).start()
     for i in (1, 2, 3, 0):
@@ -431,7 +432,7 @@
         return carry
 
     folds = channels // tall
-    ahead_folds = folds - nz // 2
+    ahead_folds = 1
     lax.fori_loop(0, ahead_folds, folding, 0)
 
     def pass_on(q):
@@ -454,7 +455,9 @@
         pass_on(q + 1)
         return folding(i, carry)
 
-    lax.fori_loop(ahead_folds, folds, folding_on, 0)
+    passed = ahead_folds + nz // 2
+    lax.fori_loop(ahead_folds, passed, folding_on, 0)
+    lax.fori_loop(passed, folds, folding, 0)
 
     def swap(v, w):
         if w < LANES:
@@ -505,6 +508,16 @@
         return carry
 
     lax.fori_loop(0, spans, part_h, 0)
+    relayed = rows_p.at[pl.ds(0, nz * (nx - 1) * width), :]
+    await_all(relayed, f_recv)
+
+    def part_p(h, carry):
+        at = pl.ds(pl.multiple_of(h * part, part), part)
+        for n, v in enumerate(partial(h, rows_p, member_p, LANES)[:3]):
+            sums[n, at, :] += v
+        return carry
+
+    lax.fori_loop(0, spans, part_p, 0)
     own_a.wait()
     await_all(send_a.at[pl.ds(0, blocks)], a_recv)
 
@@ -515,16 +528,6 @@
         return carry
 
     lax.fori_loop(0, spans, part_a, 0)
-    relayed = rows_p.at[pl.ds(0, nz * (nx - 1) * width), :]
-    await_all(relayed, f_recv)
-
-    def part_p(h, carry):
-        at = pl.ds(pl.multiple_of(h * part, part), part)
-        for n, v in enumerate(partial(h, rows_p, member_p, LANES)[:3]):
-            sums[n, at, :] += v
-        return carry
-
-    lax.fori_loop(0, spans, part_p, 0)
     await_all(send_h.at[pl.ds(0, blocks)], h_send)
     await_all(send_a.at[pl.ds(0, blocks)], a_send)
     await_all(send_p.at[pl.ds(0, last)], p_send)

time: 76.5 us -> 71.9 us (0.940)
  Pallas kernels: 74.5 us -> 69.9 us
    pallas_call x1, Pallas kernels: 73.1 us -> 68.5 us  [cross_power(): pl.pallas_call(functools.partial(kernel, cap, sizes), out_shape=jax.Shape...]
where the time goes in v5:
time: 71.9 us; the launch traced here: 71.6 us
  Pallas kernels  69.9 us (97%)
  local copies, waits for them, and re-layouts  0.8 us (1%)
    pallas_call x1, Pallas kernels, cross_power(): pl.pallas_call(functools.partial(kernel, cap, sizes), out_shape=jax.Shape...  68.5 us

profile of v5, /device:TPU:1, one launch (start us, length us, event | category | flops | bytes accessed | tf_op | source)
XLA Modules:
  0.0 71.6 jit_solution(3247196171141699485)
XLA Ops:
  0.0 1.4 %shard_map.61 = s32[1]{0:T(128)} custom-call(s32[1,2048]{1,0:T(1,128)} %bitcast.12, s32[1,2048]{1,0:T(1,128)} %bitcast.15), custom_call_target="tpu_custom_call" | custom-call | tf_op jit(solution)/shard_map/pallas_call | solution.py:726
  2.1 68.7 %conditional.1 = (f32[8,64,192]{2,1,0:T(8,128)S(1)}) conditional(s32[]{:T(128)} %bitcast.4, (s32[1]{0:T(128)}, s32[1,2048]{1,0:T(1,128)}, s32[1,2048]{1,0:T(1,128)}, bf16[2,1,8,48,2048]{4,3,2,0,1:T(8,128)(2,1)}, bf16[1536,1536]{1,0:T(8,128)(2,1)}) %tuple.20, (s32[1]{0:T(128)}, s32[1,2048]{1,0:T(1,128)}, s32[1,2048]{1,0:T(1,128)}, ...), branch_computations={%region_0.0_spmd, %region_1.0_spmd} | conditional | bytes 8 | solution.py:731
  2.3 68.5 %branch_1_fun.1 = f32[8,64,192]{2,1,0:T(8,128)S(1)} custom-call(s32[1]{0:T(128)} %get-tuple-element.46.bin_ref, s32[1,2048]{1,0:T(1,128)} %get-tuple-element.34.owner_ref, s32[1,2048]{1,0:T(1,128)} %get-tuple-element.35.size_ref, bf16[768,2048]{1,0:T(8,128)(2,1)} %bitcast.11, bf16[1536,1536]{1,0:T(8,128)(2,1)} %get-tuple-element.48.cov_hbm), custom_call_target="tpu_custom_call" | custom-call | tf_op jit(solution)/shard_map/cond/branch_1_fun/pallas_call | solution.py:641
  70.8 0.8 %copy.16 = f32[8,64,192]{2,1,0:T(8,128)} copy(f32[8,64,192]{2,1,0:T(8,128)S(1)} %get-tuple-element.38) | data formatting | bytes 786432

commit v6 on v5

--- a/solution.py
+++ b/solution.py
@@ -546,12 +546,12 @@
         else:
             acc_b[...] += term
 
-    def share_copy(source, h, to):
+    def share_copy(source, h, to, dl):
         return pltpu.make_async_remote_copy(
             src_ref=source.at[h],
             dst_ref=landed.at[lst],
             send_sem=y_send,
-            recv_sem=y_recv,
+            recv_sem=y_recv.at[dl],
             device_id=(to, chan),
             device_id_type=MESH,
         )
@@ -559,7 +559,7 @@
     def share(source, h, to):
         @pl.when(to != lst)
         def _():
-            share_copy(source, h, to).start()
+            share_copy(source, h, to, lax.rem(to - lst + nl, nl)).start()
 
         @pl.when(to == lst)
         def _():
@@ -595,10 +595,12 @@
             share(share_plus, 0, 0)
             share(share_plus, 1, 1)
             share(share_minus, 0, nl - 1)
+        if h > 2:
+            share(share_plus, h - 1, h - 1)
+            share(share_minus, h - 2, nl + 1 - h)
         finish(h)
-    for h in range(2, spans):
-        share(share_plus, h, h)
-    for h in range(1, spans):
+    share(share_plus, spans - 1, spans - 1)
+    for h in range(spans - 2, spans):
         share(share_minus, h, nl - 1 - h)
 
     row = lax.broadcasted_iota(jnp.int32, (tall_share + TAIL, part), 0)
@@ -614,9 +616,9 @@
 
     await_all(send_b.at[pl.ds(0, blocks)], b_send)
     order(lst)
-    await_all(landed.at[pl.ds(0, nl - 1)], y_recv)
-    for dl in range(1, nl):
-        order(lax.rem(lst + dl, nl))
+    for dl in sorted(range(1, nl), key=lambda d: min(d, nl - d)):
+        await_all(landed.at[0], y_recv.at[dl])
+        order(lax.rem(lst + nl - dl, nl))
     codes = [bin_land[t].astype(F32)[:1, :1] for t in range(nl)]
     for b in range(NBIN):
         total = jnp.zeros((held, part), F32)
@@ -698,7 +700,7 @@
             dma(()),
             dma(()),
             dma(()),
-            dma(()),
+            dma((nl,)),
             dma(()),
             dma(()),
         ],

time: 71.9 us -> 72.8 us (1.013)
  Pallas kernels: 69.9 us -> 70.8 us
    pallas_call x1, Pallas kernels: 68.5 us -> 69.4 us  [cross_power(): pl.pallas_call(functools.partial(kernel, cap, sizes), out_shape=jax.Shape...]
where the time goes in v6:
time: 72.8 us; the launch traced here: 72.5 us
  Pallas kernels  70.8 us (97%)
  local copies, waits for them, and re-layouts  0.8 us (1%)
    pallas_call x1, Pallas kernels, cross_power(): pl.pallas_call(functools.partial(kernel, cap, sizes), out_shape=jax.Shape...  69.4 us

profile of v6, /device:TPU:1, one launch (start us, length us, event | category | flops | bytes accessed | tf_op | source)
XLA Modules:
  0.0 72.5 jit_solution(14444986613784986953)
XLA Ops:
  0.0 1.4 %shard_map.61 = s32[1]{0:T(128)} custom-call(s32[1,2048]{1,0:T(1,128)} %bitcast.12, s32[1,2048]{1,0:T(1,128)} %bitcast.15), custom_call_target="tpu_custom_call" | custom-call | tf_op jit(solution)/shard_map/pallas_call | solution.py:728
  2.1 69.6 %conditional.1 = (f32[8,64,192]{2,1,0:T(8,128)S(1)}) conditional(s32[]{:T(128)} %bitcast.4, (s32[1]{0:T(128)}, s32[1,2048]{1,0:T(1,128)}, s32[1,2048]{1,0:T(1,128)}, bf16[2,1,8,48,2048]{4,3,2,0,1:T(8,128)(2,1)}, bf16[1536,1536]{1,0:T(8,128)(2,1)}) %tuple.20, (s32[1]{0:T(128)}, s32[1,2048]{1,0:T(1,128)}, s32[1,2048]{1,0:T(1,128)}, ...), branch_computations={%region_0.0_spmd, %region_1.0_spmd} | conditional | bytes 8 | solution.py:733
  2.3 69.4 %branch_1_fun.1 = f32[8,64,192]{2,1,0:T(8,128)S(1)} custom-call(s32[1]{0:T(128)} %get-tuple-element.46.bin_ref, s32[1,2048]{1,0:T(1,128)} %get-tuple-element.34.owner_ref, s32[1,2048]{1,0:T(1,128)} %get-tuple-element.35.size_ref, bf16[768,2048]{1,0:T(8,128)(2,1)} %bitcast.11, bf16[1536,1536]{1,0:T(8,128)(2,1)} %get-tuple-element.48.cov_hbm), custom_call_target="tpu_custom_call" | custom-call | tf_op jit(solution)/shard_map/cond/branch_1_fun/pallas_call | solution.py:643
  71.7 0.8 %copy.16 = f32[8,64,192]{2,1,0:T(8,128)} copy(f32[8,64,192]{2,1,0:T(8,128)S(1)} %get-tuple-element.38) | data formatting | bytes 786432

commit v7 on v5

--- a/solution.py
+++ b/solution.py
@@ -243,6 +243,7 @@
             lives.append(jnp.sum(live_sum.astype(F32), axis=1, keepdims=True))
         live = jnp.concatenate(lives, axis=0)
         if not first:
+            p_copy(q - 1).start()
             for i in range(nx - 1):
 
                 @pl.when(q > 1)
@@ -250,7 +251,6 @@
                     h_copy(q - 1, i).start()
 
             h_copy(q - 1, nx - 1).start()
-            p_copy(q - 1).start()
 
             @pl.when(q <= early)
             def _():
@@ -432,8 +432,7 @@
         return carry
 
     folds = channels // tall
-    ahead_folds = 1
-    lax.fori_loop(0, ahead_folds, folding, 0)
+    ahead_folds = 0
 
     def pass_on(q):
         for j in range(1, nx):

time: 71.9 us -> 71.9 us (level)
  no operation moved by 1% of the time
where the time goes in v7:
time: 71.9 us; the launch traced here: 71.6 us
  Pallas kernels  69.9 us (97%)
  local copies, waits for them, and re-layouts  0.8 us (1%)
    pallas_call x1, Pallas kernels, cross_power(): pl.pallas_call(functools.partial(kernel, cap, sizes), out_shape=jax.Shape...  68.5 us

profile of v7, /device:TPU:1, one launch (start us, length us, event | category | flops | bytes accessed | tf_op | source)
XLA Modules:
  0.0 71.6 jit_solution(10294786996783762871)
XLA Ops:
  0.0 1.4 %shard_map.61 = s32[1]{0:T(128)} custom-call(s32[1,2048]{1,0:T(1,128)} %bitcast.12, s32[1,2048]{1,0:T(1,128)} %bitcast.15), custom_call_target="tpu_custom_call" | custom-call | tf_op jit(solution)/shard_map/pallas_call | solution.py:725
  2.1 68.7 %conditional.1 = (f32[8,64,192]{2,1,0:T(8,128)S(1)}) conditional(s32[]{:T(128)} %bitcast.4, (s32[1]{0:T(128)}, s32[1,2048]{1,0:T(1,128)}, s32[1,2048]{1,0:T(1,128)}, bf16[2,1,8,48,2048]{4,3,2,0,1:T(8,128)(2,1)}, bf16[1536,1536]{1,0:T(8,128)(2,1)}) %tuple.20, (s32[1]{0:T(128)}, s32[1,2048]{1,0:T(1,128)}, s32[1,2048]{1,0:T(1,128)}, ...), branch_computations={%region_0.0_spmd, %region_1.0_spmd} | conditional | bytes 8 | solution.py:730
  2.3 68.5 %branch_1_fun.1 = f32[8,64,192]{2,1,0:T(8,128)S(1)} custom-call(s32[1]{0:T(128)} %get-tuple-element.46.bin_ref, s32[1,2048]{1,0:T(1,128)} %get-tuple-element.34.owner_ref, s32[1,2048]{1,0:T(1,128)} %get-tuple-element.35.size_ref, bf16[768,2048]{1,0:T(8,128)(2,1)} %bitcast.11, bf16[1536,1536]{1,0:T(8,128)(2,1)} %get-tuple-element.48.cov_hbm), custom_call_target="tpu_custom_call" | custom-call | tf_op jit(solution)/shard_map/cond/branch_1_fun/pallas_call | solution.py:640
  70.8 0.8 %copy.16 = f32[8,64,192]{2,1,0:T(8,128)} copy(f32[8,64,192]{2,1,0:T(8,128)S(1)} %get-tuple-element.38) | data formatting | bytes 786432
